TPU v7x, 32 devices: a whole 2x2x4 slice. The times are simulated.
32 devices in a mesh: tm: 8 (over z, x), head: 4 (over y, core).
Axes of the slice: x: 2, y: 2, z: 4, core: 2. Of those that a mesh axis runs over, the one named last changes fastest.
Arguments:
- query_rows: float32 [8192, 2048], P('tm', 'head'), may hold values from -0.125 to 0.125
- key_rows: float32 [8192, 2048], P('tm', 'head'), may hold values from -0.125 to 0.125
- value_rows: float32 [8192, 2048], P('tm', 'head'), may hold values from -1.25 to 1.25
- out_grad: float32 [8192, 2048], P('tm', 'head'), may hold values from -1.25 to 1.25
- level_weights: float32 [14, 8192], P(None, 'tm'), may hold values from 0.3 to 3
Outputs:
- query_grad: float32 [8192, 2048], P('tm', 'head')
- key_grad: float32 [8192, 2048], P('tm', 'head')
- value_grad: float32 [8192, 2048], P('tm', 'head')
- weight_grad: float32 [14, 8192], P(None, 'tm')
All inputs are finite; a program needn't handle non-finite values.
Results may differ from a plain program's by a relative error of at most 0.00011.
Values sent between devices are 32-bit elements; how exact they have to be, the bound alone decides.
No kernel may reach another device: no remote copies, remote signals or barrier semaphores. Data moves between devices by JAX's collectives and lax.ppermute only.
A program may use at most 128 MiB of HBM per device.

v0:
```python
import functools

import jax
import jax.numpy as jnp
from jax import lax
from jax.experimental import pallas as pl
from jax.experimental.pallas import tpu as pltpu
from jax.sharding import PartitionSpec as P


DK = 128
C = 128
B = 256
SUB = 8
NN = (((1,), (0,)), ((), ()))
NT = (((1,), (1,)), ((), ()))
TN = (((0,), (0,)), ((), ()))


def partner(array, axis, stride):
    return lax.ppermute(array, axis, [(i, i ^ 1 << stride) for i in range(lax.axis_size(axis))])


def split(x):
    hi = x.astype(jnp.bfloat16)
    return hi, (x - hi.astype(jnp.float32)).astype(jnp.bfloat16)


def wide(parts):
    return jnp.concatenate(parts, axis=1)


def tall(parts):
    return jnp.concatenate(parts, axis=0)


def dot(a, b, dims):
    return lax.dot_general(a, b, dims, preferred_element_type=jnp.float32)


def halves(x):
    n = x.shape[1] // 2
    return x[:, :n] + x[:, n:]


def nn(a, b):
    right = wide(b)
    return halves(dot(wide(a), tall((right, right)), NN))


def nt(a, b):
    return halves(dot(wide(a), tall((wide((b[0], b[0])), wide((b[1], b[1])))), NT))


def tn(a, b):
    right = wide(b)
    return halves(dot(tall(a), tall((right, right)), TN))


def fold(x):
    return jnp.sum(x.reshape(x.shape[0] // SUB, SUB, x.shape[1]), axis=0)


def level_table():
    s = lax.broadcasted_iota(jnp.int32, (C, C), 0)
    t = lax.broadcasted_iota(jnp.int32, (C, C), 1)
    x = jnp.bitwise_xor(s, t)
    level = jnp.zeros((C, C), jnp.int32)
    for height in range(C.bit_length() - 1):
        level = level + (x >= 1 << height).astype(jnp.int32)
    return jnp.where(s <= t, level, -1)


def state_kernel(first, bits_ref, q_hbm, k_hbm, v_hbm, d_hbm, w_ref, near_ref, send_ref, keep_ref, left_ref, right_ref, turned_ref, stage_ref, sum_ref, sems):
    heads, frames = left_ref.shape[1:3]
    half = heads // 2
    levels = send_ref.shape[0] + 1
    own = bits_ref[0]

    def copies(head):
        lanes = pl.ds(head * DK, DK)
        return [
            pltpu.make_async_copy(x.at[:, lanes], stage_ref.at[i, head], sems.at[i, head])
            for i, x in enumerate((k_hbm, q_hbm, v_hbm, d_hbm))
        ]

    def prepare(head, span):
        for i in range(2):
            x = stage_ref[i, head, span, :]
            left_ref[i, head, span, :] = wide(split(x))
            turned_ref[i, head, :, span] = x.T
            right_ref[i, head, span, :] = wide(split(stage_ref[2 + i, head, span, :]))

    def products(head, span):
        for level in range(levels):
            bit = bits_ref[level]
            row = jnp.where(bit == 1, w_ref[first + level : first + level + 1, span], 1.0)
            grown = wide(split(row * turned_ref[bit, head, :, span]))
            right = right_ref[bit, head, span, :]
            term = dot(grown, tall((right, right)), NN)
            sum_ref[head, level] = sum_ref[head, level] + term if span.start else term

    for head in range(heads):
        for copy in copies(head):
            copy.start()
    for head in range(heads + 1):
        if head < heads:
            for copy in copies(head):
                copy.wait()
        for b in range(frames // B):
            span = slice(b * B, (b + 1) * B)
            if head < heads:
                prepare(head, span)
            if head:
                products(head - 1, span)
    for head in range(heads):
        near_ref[head] = halves(sum_ref[head, 0])
    for level in range(1, levels):
        for j in range(half):
            low, high = halves(sum_ref[j, level]), halves(sum_ref[half + j, level])
            send_ref[level - 1, j] = jnp.where(own == 0, high, low)
            keep_ref[level - 1, j] = jnp.where(own == 0, low, high)


def upper_pairs(chunks):
    heights = chunks.bit_length() - 1
    return [(c, k) for c in range(chunks) for k in range(heights) if c >> k & 1]


def parts(ref, *at):
    x = ref[at]
    return x[:, :DK], x[:, DK:]


def local_kernel(heads, last, left_ref, right_ref, turned_ref, w_ref, *refs):
    start = heads[0] == 0
    if not start:
        refs = refs[6:]
    qg_ref, kg_ref, vg_ref, pr_ref, wc_ref, mix_ref = refs[:6]
    frames = left_ref.shape[2]
    chunks = frames // C
    heights = chunks.bit_length() - 1
    inner = C.bit_length()
    pairs = upper_pairs(chunks)
    spans = [slice(c * C, (c + 1) * C) for c in range(chunks)]

    if start:
        table = level_table()
        for c in range(chunks):
            mixing = jnp.zeros((C, C), jnp.float32)
            for level in range(inner):
                mixing = jnp.where(table == level, w_ref[level : level + 1, spans[c]], mixing)
            mix_ref[c] = mixing

    def add(head, ref, at, value):
        ref[at] = ref[at] + value if head else value

    def inside(head):
        lanes = slice(head * DK, (head + 1) * DK)
        sums, back = {}, {}
        for c in range(chunks - 1):
            sums[c, 0] = tn(parts(left_ref, 0, head, spans[c]), parts(right_ref, 0, head, spans[c]))
        for k in range(1, heights):
            for b in range(chunks >> k):
                if b << k < chunks - (1 << k):
                    sums[b, k] = sums[2 * b, k - 1] + sums[2 * b + 1, k - 1]

        def scores(c):
            ks, qs = parts(left_ref, 0, head, spans[c]), parts(left_ref, 1, head, spans[c])
            vs, ds = parts(right_ref, 0, head, spans[c]), parts(right_ref, 1, head, spans[c])
            gt = nt(ks, qs)
            et = nt(vs, ds)
            add(head, pr_ref, c, gt * et)
            mt = mix_ref[c]
            return split(mt * et), split(mt * gt)

        def gradients(c, me, mg):
            ks, qs = parts(left_ref, 0, head, spans[c]), parts(left_ref, 1, head, spans[c])
            vs, ds = parts(right_ref, 0, head, spans[c]), parts(right_ref, 1, head, spans[c])
            kg, vg, qg = nn(me, qs), nn(mg, ds), tn(me, ks)
            if c < chunks - 1:
                total = None
                for k in range(heights):
                    if not c >> k & 1:
                        term = back[c >> k, k]
                        total = term if total is None else total + term
                bs = split(total)
                kg = kg + nt(vs, bs)
                vg = vg + nn(ks, bs)
            kg_ref[spans[c], lanes] = kg
            vg_ref[spans[c], lanes] = vg
            ups = [k for k in range(heights) if c >> k & 1]
            if ups:
                qt = turned_ref[1, head, :, spans[c]]
                mixed = None
                for k in ups:
                    row = w_ref[inner + k : inner + k + 1, spans[c]]
                    along = nt(split(sums[(c >> k) - 1, k]), ds)
                    add(head, wc_ref, pairs.index((c, k)), fold(qt * along))
                    term = row * along
                    mixed = term if mixed is None else mixed + term
                    grad = nn(split(row * qt), ds)
                    key = ((c >> k) - 1, k)
                    back[key] = back[key] + grad if key in back else grad
                qg = qg + mixed.T
            qg_ref[spans[c], lanes] = qg

        waiting = None
        for c in reversed(range(chunks)):
            now = scores(c)
            if waiting is not None:
                gradients(c + 1, *waiting)
            waiting = now
        gradients(0, *waiting)

    for head in heads:
        inside(head)

    if last:
        wg_ref = refs[-1]
        table = level_table()
        wg_ref[...] = jnp.zeros_like(wg_ref)
        for c in range(chunks):
            product = pr_ref[c]
            for level in range(inner):
                row = jnp.sum(jnp.where(table == level, product, 0.0), axis=0, keepdims=True)
                wg_ref[level : level + 1, spans[c]] = row
        for i, (c, k) in enumerate(pairs):
            wg_ref[inner + k : inner + k + 1, spans[c]] = jnp.sum(wc_ref[i], axis=0, keepdims=True)


def received(level, head, half, own, refs):
    if level == 0:
        return refs[0][head]
    other, mine = refs[2 * level - 1], refs[2 * level]
    return jnp.where(own == head // half, mine[head % half], other[head % half])


def coarse_kernel(first, levels, final, bits_ref, right_ref, turned_ref, w_ref, qg_ref, *refs):
    count = 2 * levels.stop - 1
    arrived, refs = refs[:count], refs[count:]
    if final:
        out_hbm, wg_ref, wc_ref, out_ref, sems = refs
    else:
        out_ref, wg_ref, wc_ref = refs
    heads, frames = right_ref.shape[1:3]
    lefts = []
    for head in range(heads):
        states = []
        for level in levels:
            state = received(level, head, heads // 2, bits_ref[0], arrived)
            states.append(wide(split(jnp.where(bits_ref[level] == 1, state, 0.0))))
        lefts.append(tall(states))
    for head in range(heads):
        lanes = slice(head * DK, (head + 1) * DK)
        for c in range(frames // C):
            span = slice(c * C, (c + 1) * C)
            dh, dl = parts(right_ref, 1, head, span)
            along = halves(dot(lefts[head], tall((wide((dh, dh)), wide((dl, dl)))), NT))
            qt = turned_ref[1, head, :, span]
            mixed = None
            for i, level in enumerate(levels):
                part = along[i * DK : (i + 1) * DK, :]
                share = fold(qt * part)
                wc_ref[i, :, span] = wc_ref[i, :, span] + share if head else share
                term = w_ref[first + level : first + level + 1, span] * part
                mixed = term if mixed is None else mixed + term
            out_ref[span, lanes] = qg_ref[span, lanes] + mixed.T
        if final:
            pltpu.make_async_copy(out_ref.at[:, lanes], out_hbm.at[:, lanes], sems.at[head]).start()
    for i in range(len(levels)):
        wg_ref[i : i + 1, :] = jnp.sum(wc_ref[i], axis=0, keepdims=True)
    wg_ref[len(levels) :, :] = jnp.zeros((wg_ref.shape[0] - len(levels), frames), jnp.float32)
    if final:
        for head in range(heads):
            lanes = slice(head * DK, (head + 1) * DK)
            pltpu.make_async_copy(out_ref.at[:, lanes], out_hbm.at[:, lanes], sems.at[head]).wait()


def back_kernel(levels, times, bits_ref, left_ref, old_ref, *refs):
    arrived = refs[: 2 * levels - 1]
    out_hbm, out_ref, sems = refs[2 * levels - 1 :]
    heads, frames = left_ref.shape[1:3]
    sums = []
    for head in range(heads):
        total = None
        for level in range(levels):
            state = received(level, head, heads // 2, bits_ref[0], arrived)
            term = jnp.where(bits_ref[level] == 0, state, 0.0)
            total = term if total is None else total + term
        sums.append(split(total))
    for head in range(heads):
        lanes = slice(head * DK, (head + 1) * DK)
        for b in range(frames // B):
            span = slice(b * B, (b + 1) * B)
            out_ref[span, lanes] = old_ref[span, lanes] + times(parts(left_ref, 0, head, span), sums[head])
        pltpu.make_async_copy(out_ref.at[:, lanes], out_hbm.at[:, lanes], sems.at[head]).start()
    for head in range(heads):
        lanes = slice(head * DK, (head + 1) * DK)
        pltpu.make_async_copy(out_ref.at[:, lanes], out_hbm.at[:, lanes], sems.at[head]).wait()


def params(mib):
    return pltpu.CompilerParams(vmem_limit_bytes=mib * 2**20)


def cost(flops, size):
    return pl.CostEstimate(flops=flops, bytes_accessed=size, transcendentals=0)


def groups(heads, windows):
    count = min(heads, windows)
    rest = heads - count + 1
    return [list(range(rest))] + [[rest + i] for i in range(count - 1)]


def body(query_rows, key_rows, value_rows, out_grad, level_weights):
    frames, width = query_rows.shape
    heads = width // DK
    half = heads // 2
    levels = level_weights.shape[0]
    fine = frames.bit_length()
    device_levels = levels - fine
    far = device_levels - 1
    f32, bf16 = jnp.float32, jnp.bfloat16
    big = jax.ShapeDtypeStruct((frames, width), f32)
    kept = pltpu.VMEM((frames, width), f32)
    fine_rows = -(-fine // SUB) * SUB
    chunks = frames // C
    pairs = max(1, len(upper_pairs(chunks)))
    block = frames * width * 4
    device = lax.axis_index("tm")
    bits = jnp.bitwise_and(jnp.right_shift(device, jnp.arange(device_levels)), 1).astype(jnp.int32)
    inputs = [pltpu.with_memory_space_constraint(x, pltpu.HBM) for x in (query_rows, key_rows, value_rows, out_grad)]
    here = pl.BlockSpec(memory_space=pltpu.VMEM)
    there = pl.BlockSpec(memory_space=pl.ANY)
    scalars = pl.BlockSpec(memory_space=pltpu.SMEM)
    far_half = jax.ShapeDtypeStruct((far, half, DK, DK), f32)
    done = pltpu.SemaphoreType.DMA((heads,))

    near, send, keep, left, right, turned = pl.pallas_call(
        functools.partial(state_kernel, fine),
        in_specs=[scalars] + [there] * 4 + [here],
        out_specs=[here] * 6,
        out_shape=[
            jax.ShapeDtypeStruct((heads, DK, DK), f32),
            far_half,
            far_half,
            pltpu.VMEM((2, heads, frames, 2 * DK), bf16),
            pltpu.VMEM((2, heads, frames, 2 * DK), bf16),
            pltpu.VMEM((2, heads, DK, frames), f32),
        ],
        scratch_shapes=[
            pltpu.VMEM((4, heads, frames, DK), f32),
            pltpu.VMEM((heads, device_levels, DK, 2 * DK), f32),
            pltpu.SemaphoreType.DMA((4, heads)),
        ],
        compiler_params=params(16),
        cost_estimate=cost(10**9, 4 * block),
        name="states",
    )(bits, *inputs, level_weights)

    inner = None
    for i, group in enumerate(groups(heads, device_levels)):
        last = group[-1] == heads - 1
        shapes = [kept] * 3
        shapes += [pltpu.VMEM((chunks, C, C), f32), pltpu.VMEM((pairs, SUB, C), f32), pltpu.VMEM((chunks, C, C), f32)]
        inner = pl.pallas_call(
            functools.partial(local_kernel, group, last),
            in_specs=[here] * (10 if i else 4),
            out_specs=[here] * (7 if last else 6),
            out_shape=shapes + ([jax.ShapeDtypeStruct((fine_rows, frames), f32)] if last else []),
            input_output_aliases={4 + j: j for j in range(6)} if i else {},
            compiler_params=params(16),
            cost_estimate=cost(10**9, 7 * block // heads * len(group)),
        )(left, right, turned, level_weights, *(inner or []))
    q_local, k_local, v_local, _, _, _, w_fine = inner

    arrived = []
    carried = keep + partner(send, "tm", 0)
    for height in range(1, device_levels):
        other = partner(carried, "tm", height)
        arrived.append(other[0])
        carried = carried[1:] + other[1:]
    states = [partner(near, "tm", 0)]
    for height in range(far):
        states += [partner(arrived[height], "tm", 0), arrived[height]]

    def coarse(span, query, final):
        used = states[: 2 * span.stop - 1]
        rows = -(-len(span) // SUB) * SUB
        extra = [pltpu.VMEM((frames, width), f32), done] if final else []
        return pl.pallas_call(
            functools.partial(coarse_kernel, fine, span, final),
            in_specs=[scalars] + [here] * (4 + len(used)),
            out_specs=[there if final else here, here],
            out_shape=[big if final else kept, jax.ShapeDtypeStruct((rows, frames), f32)],
            scratch_shapes=[pltpu.VMEM((len(span), SUB, frames), f32)] + extra,
            input_output_aliases={} if final else {4: 0},
            compiler_params=params(16),
            cost_estimate=cost(10**9, 2 * block),
            name="coarse",
        )(bits, right, turned, level_weights, query, *used)

    w_terms = [w_fine[:fine]]
    if far:
        q_local, w_early = coarse(range(far), q_local, False)
        w_terms.append(w_early[:far])
    q_total, w_late = coarse(range(far, device_levels), q_local, True)
    w_terms.append(w_late[:1])

    weight_grad = jnp.concatenate(w_terms, axis=0)
    for height in range(lax.axis_size("head").bit_length() - 1):
        weight_grad = weight_grad + partner(weight_grad, "head", height)

    totals = []
    for times, operand, old in ((nt, right, k_local), (nn, left, v_local)):
        totals.append(
            pl.pallas_call(
                functools.partial(back_kernel, device_levels, times),
                in_specs=[scalars] + [here] * (2 + len(states)),
                out_specs=there,
                out_shape=big,
                scratch_shapes=[pltpu.VMEM((frames, width), f32), done],
                compiler_params=params(16),
                cost_estimate=cost(10**9, 2 * block),
            )(bits, operand, old, *states)
        )
    return (q_total, *totals, weight_grad)


def solution(mesh):
    in_specs = (P("tm", "head"), P("tm", "head"), P("tm", "head"), P("tm", "head"), P(None, "tm"))
    out_specs = (P("tm", "head"), P("tm", "head"), P("tm", "head"), P(None, "tm"))
    return jax.shard_map(body, mesh=mesh, in_specs=in_specs, out_specs=out_specs, check_vma=False)
```

profile of v0, /device:TPU:1, one launch (start us, length us, event | category | flops | bytes accessed | tf_op | source)
XLA Modules:
  0.0 53.4 jit_solution(14354946884010448508)
XLA Ops:
  0.6 0.0 copy-start
  0.7 0.8 %copy-done = f32[14,1024]{1,0:T(8,128)S(1)} copy-done((f32[14,1024]{1,0:T(8,128)S(1)}, f32[14,1024]{1,0:T(8,128)}, u32[]{:S(2)}) %copy-start) | copy-done | bytes 57368
  1.5 7.0 %states.1 = (f32[4,128,128]{2,1,0:T(8,128)S(1)}, f32[2,2,128,128]{3,2,1,0:T(8,128)S(1)}, f32[2,2,128,128]{3,2,1,0:T(8,128)S(1)}, bf16[2,4,1024,256]{3,2,1,0:T(8,...) custom-call(s32[3]{0:T(128)S(1)} %shift-right-arithmetic_and_fusion.bits_ref, ...), custom_call_target="tpu_custom_call" | custom-call | flops 1000000000 | bytes 8388608 | tf_op jit(solution)/shard_map/states/pallas_call | solution.py:341
  8.5 2.1 %collective-permute-start.1 = (f32[2,2,128,128]{3,2,1,0:T(8,128)S(1)}, f32[2,2,128,128]{3,2,1,0:T(8,128)S(1)}, u32[]{:S(2)}, u32[]{:S(2)}) collective-permute-start(f32[2,2,128,128]{3,2,1,0:T(8,128)S(1)} %get-tuple-element.48), channel_id=1, source_target_pairs={{0,4},{4,0},{8,12},{12,8},{16,20},{20,16},{24,28},{28,24},{1,5},{5... | collective-permute-start | bytes 786440 | tf_op jit(solution)/shard_map/ppermute | solution.py:21
  10.6 6.0 %collective-permute-done.1 = f32[2,2,128,128]{3,2,1,0:T(8,128)S(1)} collective-permute-done((f32[2,2,128,128]{3,2,1,0:T(8,128)S(1)}, f32[2,2,128,128]{3,2,1,0:T(8,128)S(1)}, u32[]{:S(2)}, u32[]{:S(2)}) %collective-permute-start.1) | collective-permute-done | bytes 262176 | tf_op jit(solution)/shard_map/ppermute | solution.py:21
  16.6 1.3 %collective-permute-start.2 = (f32[2,2,128,128]{3,2,1,0:T(8,128)S(1)}, f32[2,2,128,128]{3,2,1,0:T(8,128)S(1)}, u32[]{:S(2)}, u32[]{:S(2)}) collective-permute-start(f32[2,2,128,128]{3,2,1,0:T(8,128)S(1)} %add.12), channel_id=1, source_target_pairs={{0,8},{4,12},{8,0},{12,4},{16,24},{20,28},{24,16},{28,20},{1,9},{5... | collective-permute-start | bytes 786440 | tf_op jit(solution)/shard_map/ppermute | solution.py:21
  17.9 1.2 %collective-permute-start = (f32[4,128,128]{2,1,0:T(8,128)S(1)}, f32[4,128,128]{2,1,0:T(8,128)S(1)}, u32[]{:S(2)}, u32[]{:S(2)}) collective-permute-start(f32[4,128,128]{2,1,0:T(8,128)S(1)} %get-tuple-element.46), channel_id=1, source_target_pairs={{0,4},{4,0},{8,12},{12,8},{16,20},{20,16},{24,28},{28,24},{1,5},{5... | collective-permute-start | bytes 786440 | tf_op jit(solution)/shard_map/ppermute | solution.py:21
  19.2 4.1 %collective-permute-done.2 = f32[2,2,128,128]{3,2,1,0:T(8,128)S(1)} collective-permute-done((f32[2,2,128,128]{3,2,1,0:T(8,128)S(1)}, f32[2,2,128,128]{3,2,1,0:T(8,128)S(1)}, u32[]{:S(2)}, u32[]{:S(2)}) %collective-permute-start.2) | collective-permute-done | bytes 262176 | tf_op jit(solution)/shard_map/ppermute | solution.py:21
  23.3 2.1 %collective-permute-start.4 = (f32[1,2,128,128]{3,2,1,0:T(8,128)S(1)}, f32[1,2,128,128]{3,2,1,0:T(8,128)S(1)}, u32[]{:S(2)}, u32[]{:S(2)}) collective-permute-start(f32[1,2,128,128]{3,2,1,0:T(8,128)S(1)} %get-tuple-element.56), channel_id=1, source_target_pairs={{0,16},{4,20},{8,24},{12,28},{16,0},{20,4},{24,8},{28,12},{1,17},{... | collective-permute-start | bytes 393224 | tf_op jit(solution)/shard_map/ppermute | solution.py:21
  25.4 5.1 %shard_map.84 = (f32[1024,512]{1,0:T(8,128)S(1)}, f32[1024,512]{1,0:T(8,128)S(1)}, f32[1024,512]{1,0:T(8,128)S(1)}, f32[8,128,128]{2,1,0:T(8,128)S(1)}, f32[12,8...) custom-call(bf16[2,4,1024,256]{3,2,1,0:T(8,128)(2,1)S(1)} %get-tuple-element.32.left_ref, ...), custom_call_target="tpu_custom_call" | custom-call | flops 1000000000 | bytes 7340032 | tf_op jit(solution)/shard_map/pallas_call | solution.py:368
  30.5 1.3 %collective-permute-start.3 = (f32[2,128,128]{2,1,0:T(8,128)S(1)}, f32[2,128,128]{2,1,0:T(8,128)S(1)}, u32[]{:S(2)}, u32[]{:S(2)}) collective-permute-start(f32[2,128,128]{2,1,0:T(8,128)S(1)} %get-tuple-element.57.refs_2_), channel_id=1, source_target_pairs={{0,4},{4,0},{8,12},{12,8},{16,20},{20,16},{24,28},{28,24},{1,5},{5... | collective-permute-start | bytes 393224 | tf_op jit(solution)/shard_map/ppermute | solution.py:21
  31.8 2.7 %shard_map.85 = (f32[1024,512]{1,0:T(8,128)S(1)}, f32[1024,512]{1,0:T(8,128)S(1)}, f32[1024,512]{1,0:T(8,128)S(1)}, f32[8,128,128]{2,1,0:T(8,128)S(1)}, f32[12,8...) custom-call(bf16[2,4,1024,256]{3,2,1,0:T(8,128)(2,1)S(1)} %get-tuple, ...), custom_call_target="tpu_custom_call", output_to_operand_aliasing={{0}: (4, {}), {1}: (5, {}), {2}: (6, {}), {3}: (7, {}), {4}... | custom-call | flops 1000000000 | bytes 3670016 | tf_op jit(solution)/shard_map/pallas_call | solution.py:368
  34.5 0.0 collective-permute-done.4
  34.5 0.3 collective-permute-start.5
  34.8 2.9 %shard_map.86 = (f32[1024,512]{1,0:T(8,128)S(1)}, f32[1024,512]{1,0:T(8,128)S(1)}, f32[1024,512]{1,0:T(8,128)S(1)}, f32[8,128,128]{2,1,0:T(8,128)S(1)}, f32[12,8...) custom-call(bf16[2,4,1024,256]{3,2,1,0:T(8,128)(2,1)S(1)} %get-tuple, ...), custom_call_target="tpu_custom_call", output_to_operand_aliasing={{0}: (4, {}), {1}: (5, {}), {2}: (6, {}), {3}: (7, {}), {4}... | custom-call | flops 1000000000 | bytes 3670016 | tf_op jit(solution)/shard_map/pallas_call | solution.py:368
  37.7 0.0 collective-permute-done.refs_0_
  37.7 0.0 collective-permute-done.3.refs_1_
  37.8 2.6 %coarse.2 = (f32[1024,512]{1,0:T(8,128)S(1)}, f32[8,1024]{1,0:T(8,128)S(1)}) custom-call(s32[3]{0:T(128)S(1)} %shift-right-arithmetic_and_fusion.bits_ref, bf16[2,4,1024,256]{3,2,1,0:T(8,128)(2,1)S(1)} %get-tuple-element.30.right_ref.left_ref, f32[2,4,128,1024]{3,2,1,0:T(8,128)S(1)} %get-tuple-element.31.turned_ref, ...), custom_call_target="tpu_custom_call", output_to_operand_aliasing={{0}: (4, {})} | custom-call | flops 1000000000 | bytes 4194304 | tf_op jit(solution)/shard_map/coarse/pallas_call | solution.py:393
  40.4 0.0 collective-permute-done.5.refs_3_
  40.4 3.1 %coarse.3 = (f32[1024,512]{1,0:T(8,128)}, f32[8,1024]{1,0:T(8,128)S(1)}) custom-call(s32[3]{0:T(128)S(1)} %shift-right-arithmetic_and_fusion.bits_ref, bf16[2,4,1024,256]{3,2,1,0:T(8,128)(2,1)S(1)} %get-tuple-element.30.right_ref.left_ref, f32[2,4,128,1024]{3,2,1,0:T(8,128)S(1)} %get-tuple-element.31.turned_ref, f32[14,1024]{1,0:T(8,128)S(1)} %copy-done, ...), custom_call_target="tpu_custom_call" | custom-call | flops 1000000000 | bytes 4194304 | tf_op jit(solution)/shard_map/coarse/pallas_call | solution.py:393
  43.5 3.3 %collective-permute-start.6 = (f32[14,1024]{1,0:T(8,128)S(1)}, f32[14,1024]{1,0:T(8,128)S(1)}, u32[]{:S(2)}, u32[]{:S(2)}) collective-permute-start(f32[14,1024]{1,0:T(8,128)S(1)} %pad_maximum_fusion), channel_id=1, source_target_pairs={{0,1},{1,0},{2,3},{3,2},{4,5},{5,4},{6,7},{7,6},{8,9},{9,8},{10,11... | collective-permute-start | bytes 172040 | tf_op jit(solution)/shard_map/ppermute | solution.py:21
  46.8 2.2 %shard_map.88 = f32[1024,512]{1,0:T(8,128)} custom-call(s32[3]{0:T(128)S(1)} %shift-right-arithmetic_and_fusion.bits_ref, bf16[2,4,1024,256]{3,2,1,0:T(8,128)(2,1)S(1)} %get-tuple-element.32.left_ref, f32[1024,512]{1,0:T(8,128)S(1)} %get-tuple-element.52.old_ref, f32[4,128,128]{2,1,0:T(8,128)S(1)} %collective-permute-done.refs_0_, ...), custom_call_target="tpu_custom_call" | custom-call | flops 1000000000 | bytes 4194304 | tf_op jit(solution)/shard_map/pallas_call | solution.py:419
  49.0 0.0 collective-permute-done.6
  49.1 1.3 %collective-permute-start.7 = (f32[14,1024]{1,0:T(8,128)S(1)}, f32[14,1024]{1,0:T(8,128)S(1)}, u32[]{:S(2)}, u32[]{:S(2)}) collective-permute-start(f32[14,1024]{1,0:T(8,128)S(1)} %fusion), channel_id=1, source_target_pairs={{0,2},{1,3},{2,0},{3,1},{4,6},{5,7},{6,4},{7,5},{8,10},{9,11},{10,... | collective-permute-start | bytes 172040 | tf_op jit(solution)/shard_map/ppermute | solution.py:21
  50.4 2.2 %shard_map.87 = f32[1024,512]{1,0:T(8,128)} custom-call(s32[3]{0:T(128)S(1)} %shift-right-arithmetic_and_fusion.bits_ref, bf16[2,4,1024,256]{3,2,1,0:T(8,128)(2,1)S(1)} %get-tuple-element.30.right_ref.left_ref, f32[1024,512]{1,0:T(8,128)S(1)} %get-tuple-element.51.old_ref, f32[4,128,128]{2,1,0:T(8,128)S(1)} %collective-permute-done.refs_0_, ...), custom_call_target="tpu_custom_call" | custom-call | flops 1000000000 | bytes 4194304 | tf_op jit(solution)/shard_map/pallas_call | solution.py:419
  52.6 0.1 collective-permute-done.7
  52.8 0.6 %add.15 = f32[14,1024]{1,0:T(8,128)} add(f32[14,1024]{1,0:T(8,128)S(1)} %fusion, f32[14,1024]{1,0:T(8,128)S(1)} %collective-permute-done.7) | non-fusion elementwise | flops 14336 | bytes 172032 | tf_op jit(solution)/shard_map/add | solution.py:414
  (7 shorter events, 0.1 us)
Async XLA Ops:
  0.6 0.8 %copy-start = (f32[14,1024]{1,0:T(8,128)S(1)}, f32[14,1024]{1,0:T(8,128)}, u32[]{:S(2)}) copy-start(f32[14,1024]{1,0:T(8,128)} %w_ref.11) | copy-start | bytes 172036
  8.5 8.1 %collective-permute-start.1 = (f32[2,2,128,128]{3,2,1,0:T(8,128)S(1)}, f32[2,2,128,128]{3,2,1,0:T(8,128)S(1)}, u32[]{:S(2)}, u32[]{:S(2)}) collective-permute-start(f32[2,2,128,128]{3,2,1,0:T(8,128)S(1)} %get-tuple-element.48), channel_id=1, source_target_pairs={{0,4},{4,0},{8,12},{12,8},{16,20},{20,16},{24,28},{28,24},{1,5},{5... | collective-permute-start | bytes 786440 | tf_op jit(solution)/shard_map/ppermute | solution.py:21
  16.6 6.7 %collective-permute-start.2 = (f32[2,2,128,128]{3,2,1,0:T(8,128)S(1)}, f32[2,2,128,128]{3,2,1,0:T(8,128)S(1)}, u32[]{:S(2)}, u32[]{:S(2)}) collective-permute-start(f32[2,2,128,128]{3,2,1,0:T(8,128)S(1)} %add.12), channel_id=1, source_target_pairs={{0,8},{4,12},{8,0},{12,4},{16,24},{20,28},{24,16},{28,20},{1,9},{5... | collective-permute-start | bytes 786440 | tf_op jit(solution)/shard_map/ppermute | solution.py:21
  17.9 19.8 %collective-permute-start = (f32[4,128,128]{2,1,0:T(8,128)S(1)}, f32[4,128,128]{2,1,0:T(8,128)S(1)}, u32[]{:S(2)}, u32[]{:S(2)}) collective-permute-start(f32[4,128,128]{2,1,0:T(8,128)S(1)} %get-tuple-element.46), channel_id=1, source_target_pairs={{0,4},{4,0},{8,12},{12,8},{16,20},{20,16},{24,28},{28,24},{1,5},{5... | collective-permute-start | bytes 786440 | tf_op jit(solution)/shard_map/ppermute | solution.py:21
  23.3 11.2 %collective-permute-start.4 = (f32[1,2,128,128]{3,2,1,0:T(8,128)S(1)}, f32[1,2,128,128]{3,2,1,0:T(8,128)S(1)}, u32[]{:S(2)}, u32[]{:S(2)}) collective-permute-start(f32[1,2,128,128]{3,2,1,0:T(8,128)S(1)} %get-tuple-element.56), channel_id=1, source_target_pairs={{0,16},{4,20},{8,24},{12,28},{16,0},{20,4},{24,8},{28,12},{1,17},{... | collective-permute-start | bytes 393224 | tf_op jit(solution)/shard_map/ppermute | solution.py:21
  30.5 7.2 %collective-permute-start.3 = (f32[2,128,128]{2,1,0:T(8,128)S(1)}, f32[2,128,128]{2,1,0:T(8,128)S(1)}, u32[]{:S(2)}, u32[]{:S(2)}) collective-permute-start(f32[2,128,128]{2,1,0:T(8,128)S(1)} %get-tuple-element.57.refs_2_), channel_id=1, source_target_pairs={{0,4},{4,0},{8,12},{12,8},{16,20},{20,16},{24,28},{28,24},{1,5},{5... | collective-permute-start | bytes 393224 | tf_op jit(solution)/shard_map/ppermute | solution.py:21
  34.5 5.9 %collective-permute-start.5 = (f32[2,128,128]{2,1,0:T(8,128)S(1)}, f32[2,128,128]{2,1,0:T(8,128)S(1)}, u32[]{:S(2)}, u32[]{:S(2)}) collective-permute-start(f32[2,128,128]{2,1,0:T(8,128)S(1)} %bitcast.4), channel_id=1, source_target_pairs={{0,4},{4,0},{8,12},{12,8},{16,20},{20,16},{24,28},{28,24},{1,5},{5... | collective-permute-start | bytes 393224 | tf_op jit(solution)/shard_map/ppermute | solution.py:21
  43.5 5.5 %collective-permute-start.6 = (f32[14,1024]{1,0:T(8,128)S(1)}, f32[14,1024]{1,0:T(8,128)S(1)}, u32[]{:S(2)}, u32[]{:S(2)}) collective-permute-start(f32[14,1024]{1,0:T(8,128)S(1)} %pad_maximum_fusion), channel_id=1, source_target_pairs={{0,1},{1,0},{2,3},{3,2},{4,5},{5,4},{6,7},{7,6},{8,9},{9,8},{10,11... | collective-permute-start | bytes 172040 | tf_op jit(solution)/shard_map/ppermute | solution.py:21
  49.1 3.7 %collective-permute-start.7 = (f32[14,1024]{1,0:T(8,128)S(1)}, f32[14,1024]{1,0:T(8,128)S(1)}, u32[]{:S(2)}, u32[]{:S(2)}) collective-permute-start(f32[14,1024]{1,0:T(8,128)S(1)} %fusion), channel_id=1, source_target_pairs={{0,2},{1,3},{2,0},{3,1},{4,6},{5,7},{6,4},{7,5},{8,10},{9,11},{10,... | collective-permute-start | bytes 172040 | tf_op jit(solution)/shard_map/ppermute | solution.py:21
where the time goes:
time: 54.4 us; the launch traced here: 53.4 us
  Pallas kernels  27.9 us (51%)
  starting transfers between devices  12.9 us (24%)
  waiting for transfers between devices  10.3 us (19%)
  local copies, waits for them, and re-layouts  0.84 us (2%)
  between operations  0.78 us (1%)
  other arithmetic  0.74 us (1%)
    ppermute x8, starting transfers between devices, partner(): lax.ppermute(array, axis, [(i, i ^ 1 << stride) for i in range(lax.axis_s...  12.9 us
    pallas_call x3, Pallas kernels, body(): pl.pallas_call(functools.partial(local_kernel, group, last), in_specs=[he...  10.7 us
    ppermute x8, waiting for transfers between devices, partner(): lax.ppermute(array, axis, [(i, i ^ 1 << stride) for i in range(lax.axis_s...  10.3 us
    pallas_call x1, Pallas kernels, body(): pl.pallas_call(functools.partial(state_kernel, fine), in_specs=[scalars]...  6.97 us
    pallas_call x2, Pallas kernels, coarse(): pl.pallas_call(functools.partial(coarse_kernel, fine, span, final), in_sp...  5.68 us
    pallas_call x2, Pallas kernels, body(): pl.pallas_call(functools.partial(back_kernel, device_levels, times), in_s...  4.45 us
  transfers between devices with their start and end apart: 8, of which 3 were waited for; matrix products, arithmetic and copies ran while one was open for 0% of the time, Pallas kernels for 33%

commit v1 on v0

v1 whole, which is shorter than its diff:
```python
import functools

import jax
import jax.numpy as jnp
from jax import lax
from jax.experimental import pallas as pl
from jax.experimental.pallas import tpu as pltpu
from jax.sharding import PartitionSpec as P


DK = 128
C = 128
B = 256
SUB = 8
NN = (((1,), (0,)), ((), ()))
NT = (((1,), (1,)), ((), ()))
TN = (((0,), (0,)), ((), ()))


def partner(array, axis, stride):
    return lax.ppermute(array, axis, [(i, i ^ 1 << stride) for i in range(lax.axis_size(axis))])


def split(x):
    hi = x.astype(jnp.bfloat16)
    return hi, (x - hi.astype(jnp.float32)).astype(jnp.bfloat16)


def wide(parts):
    return jnp.concatenate(parts, axis=1)


def tall(parts):
    return jnp.concatenate(parts, axis=0)


def dot(a, b, dims):
    return lax.dot_general(a, b, dims, preferred_element_type=jnp.float32)


def halves(x):
    n = x.shape[1] // 2
    return x[:, :n] + x[:, n:]


def nn(a, b):
    right = wide(b)
    return halves(dot(wide(a), tall((right, right)), NN))


def nt(a, b):
    return halves(dot(wide(a), tall((wide((b[0], b[0])), wide((b[1], b[1])))), NT))


def tn(a, b):
    right = wide(b)
    return halves(dot(tall(a), tall((right, right)), TN))


def fold(x):
    return jnp.sum(x.reshape(x.shape[0] // SUB, SUB, x.shape[1]), axis=0)


def level_table():
    s = lax.broadcasted_iota(jnp.int32, (C, C), 0)
    t = lax.broadcasted_iota(jnp.int32, (C, C), 1)
    x = jnp.bitwise_xor(s, t)
    level = jnp.zeros((C, C), jnp.int32)
    for height in range(C.bit_length() - 1):
        level = level + (x >= 1 << height).astype(jnp.int32)
    return jnp.where(s <= t, level, -1)


def bit_of(level):
    return jnp.bitwise_and(jnp.right_shift(lax.axis_index("tm"), level), 1)


def state_kernel(first, q_hbm, k_hbm, v_hbm, d_hbm, w_hbm, near_ref, send_ref, keep_ref, left_ref, right_refs, turned_refs, w_ref, stage_ref, sum_ref, sems, w_sem):
    heads, frames = left_ref.shape[1:3]
    half = heads // 2
    levels = send_ref.shape[0] + 1
    own = bit_of(0)

    def copies(head):
        lanes = pl.ds(head * DK, DK)
        return [
            pltpu.make_async_copy(x.at[:, lanes], stage_ref.at[i, head], sems.at[i, head])
            for i, x in enumerate((k_hbm, q_hbm, v_hbm, d_hbm))
        ]

    def prepare(head, span):
        for i in range(2):
            x = stage_ref[i, head, span, :]
            left_ref[i, head, span, :] = wide(split(x))
            turned_refs[head % 2][i, head // 2, :, span] = x.T
            right_refs[head % 2][i, head // 2, span, :] = wide(split(stage_ref[2 + i, head, span, :]))

    def products(head, span):
        for level in range(levels):
            bit = bit_of(level)
            row = jnp.where(bit == 1, w_ref[first + level : first + level + 1, span], 1.0)
            grown = wide(split(row * turned_refs[head % 2][bit, head // 2, :, span]))
            right = right_refs[head % 2][bit, head // 2, span, :]
            term = dot(grown, tall((right, right)), NN)
            sum_ref[head, level] = sum_ref[head, level] + term if span.start else term

    weights = pltpu.make_async_copy(w_hbm, w_ref, w_sem)
    for head in range(heads):
        for copy in copies(head):
            copy.start()
        if head == 0:
            weights.start()
    for head in range(heads + 1):
        if head < heads:
            for copy in copies(head):
                copy.wait()
        if head == 1:
            weights.wait()
        for b in range(frames // B):
            span = slice(b * B, (b + 1) * B)
            if head < heads:
                prepare(head, span)
            if head:
                products(head - 1, span)
    for head in range(heads):
        near_ref[head] = halves(sum_ref[head, 0])
    for level in range(1, levels):
        for j in range(half):
            low, high = halves(sum_ref[j, level]), halves(sum_ref[half + j, level])
            send_ref[level - 1, j] = jnp.where(own == 0, high, low)
            keep_ref[level - 1, j] = jnp.where(own == 0, low, high)


def upper_pairs(chunks):
    heights = chunks.bit_length() - 1
    return [(c, k) for c in range(chunks) for k in range(heights) if c >> k & 1]


def parts(ref, *at):
    x = ref[at]
    return x[:, :DK], x[:, DK:]


def local_kernel(heads, last, left_ref, right_refs, turned_refs, w_ref, *refs):
    start = heads[0] == 0
    if not start:
        refs = refs[7:]
    qg_ref, kg_ref, vg_ref, pr_ref, wc_ref, mix_ref, col_ref = refs[:7]
    frames = left_ref.shape[2]
    chunks = frames // C
    heights = chunks.bit_length() - 1
    inner = C.bit_length()
    pairs = upper_pairs(chunks)
    spans = [slice(c * C, (c + 1) * C) for c in range(chunks)]

    if start:
        table = level_table()
        for c in range(chunks):
            mixing = jnp.zeros((C, C), jnp.float32)
            for level in range(inner):
                mixing = jnp.where(table == level, w_ref[level : level + 1, spans[c]], mixing)
            mix_ref[c] = mixing
            for i in range(col_ref.shape[0]):
                level = inner + heights + i
                col_ref[i, spans[c], :] = jnp.broadcast_to(w_ref[level : level + 1, spans[c]], (C, C)).T

    def right(i, head, span):
        return parts(right_refs[head % 2], i, head // 2, span)

    def add(head, ref, at, value):
        ref[at] = ref[at] + value if head else value

    def inside(head):
        lanes = slice(head * DK, (head + 1) * DK)
        sums, back = {}, {}
        for c in range(chunks - 1):
            sums[c, 0] = tn(parts(left_ref, 0, head, spans[c]), right(0, head, spans[c]))
        for k in range(1, heights):
            for b in range(chunks >> k):
                if b << k < chunks - (1 << k):
                    sums[b, k] = sums[2 * b, k - 1] + sums[2 * b + 1, k - 1]

        def scores(c):
            ks, qs = parts(left_ref, 0, head, spans[c]), parts(left_ref, 1, head, spans[c])
            vs, ds = right(0, head, spans[c]), right(1, head, spans[c])
            gt = nt(ks, qs)
            et = nt(vs, ds)
            add(head, pr_ref, c, gt * et)
            mt = mix_ref[c]
            return split(mt * et), split(mt * gt)

        def gradients(c, me, mg):
            ks, qs = parts(left_ref, 0, head, spans[c]), parts(left_ref, 1, head, spans[c])
            vs, ds = right(0, head, spans[c]), right(1, head, spans[c])
            kg, vg, qg = nn(me, qs), nn(mg, ds), tn(me, ks)
            if c < chunks - 1:
                total = None
                for k in range(heights):
                    if not c >> k & 1:
                        term = back[c >> k, k]
                        total = term if total is None else total + term
                bs = split(total)
                kg = kg + nt(vs, bs)
                vg = vg + nn(ks, bs)
            kg_ref[spans[c], lanes] = kg
            vg_ref[spans[c], lanes] = vg
            ups = [k for k in range(heights) if c >> k & 1]
            if ups:
                qt = turned_refs[head % 2][1, head // 2, :, spans[c]]
                mixed = None
                for k in ups:
                    row = w_ref[inner + k : inner + k + 1, spans[c]]
                    along = nt(split(sums[(c >> k) - 1, k]), ds)
                    add(head, wc_ref, pairs.index((c, k)), fold(qt * along))
                    term = row * along
                    mixed = term if mixed is None else mixed + term
                    grad = nn(split(row * qt), ds)
                    key = ((c >> k) - 1, k)
                    back[key] = back[key] + grad if key in back else grad
                qg = qg + mixed.T
            qg_ref[spans[c], lanes] = qg

        waiting = None
        for c in reversed(range(chunks)):
            now = scores(c)
            if waiting is not None:
                gradients(c + 1, *waiting)
            waiting = now
        gradients(0, *waiting)

    for head in heads:
        inside(head)

    if last:
        wg_ref = refs[7]
        table = level_table()
        wg_ref[...] = jnp.zeros_like(wg_ref)
        for c in range(chunks):
            product = pr_ref[c]
            for level in range(inner):
                row = jnp.sum(jnp.where(table == level, product, 0.0), axis=0, keepdims=True)
                wg_ref[level : level + 1, spans[c]] = row
        for i, (c, k) in enumerate(pairs):
            wg_ref[inner + k : inner + k + 1, spans[c]] = jnp.sum(wc_ref[i], axis=0, keepdims=True)


def received(level, head, half, refs):
    if level == 0:
        return refs[0][head]
    other, mine = refs[2 * level - 1], refs[2 * level]
    return jnp.where(bit_of(0) == head // half, mine[head % half], other[head % half])


def coarse_kernel(first, levels, left_ref, right_refs, col_ref, old_q, old_w, *refs):
    count = 2 * levels.stop - 1
    arrived = refs[:count]
    out_ref, wg_ref, product_ref = refs[count:]
    heads, frames = left_ref.shape[1:3]
    for head in range(heads):
        lanes = slice(head * DK, (head + 1) * DK)
        states = []
        for level in levels:
            state = received(level, head, heads // 2, arrived)
            states.append(split(jnp.where(bit_of(level) == 1, state, 0.0)))
        for b in range(frames // B):
            span = slice(b * B, (b + 1) * B)
            ds = parts(right_refs[head % 2], 1, head // 2, span)
            qh, ql = parts(left_ref, 1, head, span)
            q = qh.astype(jnp.float32) + ql.astype(jnp.float32)
            mixed = old_q[span, lanes]
            for i, level in enumerate(levels):
                along = nt(ds, states[i])
                product_ref[i, span, :] = product_ref[i, span, :] + q * along if head else q * along
                mixed = mixed + col_ref[level, span, :] * along
            out_ref[span, lanes] = mixed
    for i, level in enumerate(levels):
        for c in range(frames // C):
            span = slice(c * C, (c + 1) * C)
            row = jnp.sum(product_ref[i, span, :].T, axis=0, keepdims=True)
            wg_ref[first + level : first + level + 1, span] = row


def back_kernel(levels, times, operand, extra, *refs):
    if operand == "left":
        factor = lambda head, span, ref: parts(ref, 0, head, span)
        factor_refs, refs = refs[0], refs[1:]
    else:
        factor = lambda head, span, refs: parts(refs[head % 2], 0, head // 2, span)
        factor_refs, refs = refs[0], refs[1:]
    old_ref, refs = refs[0], refs[1:]
    whole = []
    if extra:
        done_ref, refs = refs[0], refs[1:]
    arrived, refs = refs[: 2 * levels - 1], refs[2 * levels - 1 :]
    out_hbm, refs = refs[0], refs[1:]
    if extra:
        done_hbm, refs = refs[0], refs[1:]
    out_ref, sems = refs
    frames, width = old_ref.shape
    heads = width // DK
    blocks = frames // B
    if extra:
        whole = [pltpu.make_async_copy(done_ref, done_hbm, sems.at[heads, 0])]
        whole[0].start()

    def copy(head, b):
        at = (slice(b * B, (b + 1) * B), slice(head * DK, (head + 1) * DK))
        return pltpu.make_async_copy(out_ref.at[at], out_hbm.at[at], sems.at[head, b])

    for head in range(heads):
        lanes = slice(head * DK, (head + 1) * DK)
        total = None
        for level in range(levels):
            state = received(level, head, heads // 2, arrived)
            term = jnp.where(bit_of(level) == 0, state, 0.0)
            total = term if total is None else total + term
        bs = split(total)
        for b in range(blocks):
            span = slice(b * B, (b + 1) * B)
            out_ref[span, lanes] = old_ref[span, lanes] + times(factor(head, span, factor_refs), bs)
            copy(head, b).start()
    for head in range(heads):
        for b in range(blocks):
            copy(head, b).wait()
    for item in whole:
        item.wait()


def params(mib):
    return pltpu.CompilerParams(vmem_limit_bytes=mib * 2**20)


def cost(flops, size):
    return pl.CostEstimate(flops=flops, bytes_accessed=size, transcendentals=0)


def groups(heads, windows):
    count = min(heads, windows)
    rest = heads - count + 1
    return [list(range(rest))] + [[rest + i] for i in range(count - 1)]


def body(query_rows, key_rows, value_rows, out_grad, level_weights):
    frames, width = query_rows.shape
    heads = width // DK
    half = heads // 2
    levels = level_weights.shape[0]
    fine = frames.bit_length()
    device_levels = levels - fine
    far = device_levels - 1
    f32, bf16 = jnp.float32, jnp.bfloat16
    big = jax.ShapeDtypeStruct((frames, width), f32)
    kept = pltpu.VMEM((frames, width), f32)
    chunks = frames // C
    pairs = max(1, len(upper_pairs(chunks)))
    block = frames * width * 4
    here = pl.BlockSpec(memory_space=pltpu.VMEM)
    there = pl.BlockSpec(memory_space=pl.ANY)
    inputs = [pltpu.with_memory_space_constraint(x, pltpu.HBM) for x in (query_rows, key_rows, value_rows, out_grad, level_weights)]
    far_half = jax.ShapeDtypeStruct((far, half, DK, DK), f32)
    rows = -(-levels // SUB) * SUB

    near, send, keep, left, right, turned = pl.pallas_call(
        functools.partial(state_kernel, fine),
        in_specs=[there] * 5,
        out_specs=[here] * 4 + [[here] * 2] * 2,
        out_shape=[
            jax.ShapeDtypeStruct((heads, DK, DK), f32),
            far_half,
            far_half,
            pltpu.VMEM((2, heads, frames, 2 * DK), bf16),
            [pltpu.VMEM((2, half, frames, 2 * DK), bf16)] * 2,
            [pltpu.VMEM((2, half, DK, frames), f32)] * 2,
        ],
        scratch_shapes=[
            pltpu.VMEM((levels, frames), f32),
            pltpu.VMEM((4, heads, frames, DK), f32),
            pltpu.VMEM((heads, device_levels, DK, 2 * DK), f32),
            pltpu.SemaphoreType.DMA((4, heads)),
            pltpu.SemaphoreType.DMA,
        ],
        compiler_params=params(16),
        cost_estimate=cost(10**9, 4 * block),
        name="states",
    )(*inputs)

    inner = None
    for i, group in enumerate(groups(heads, device_levels)):
        last = group[-1] == heads - 1
        shapes = [kept] * 3
        shapes += [pltpu.VMEM((chunks, C, C), f32), pltpu.VMEM((pairs, SUB, C), f32), pltpu.VMEM((chunks, C, C), f32)]
        shapes.append(pltpu.VMEM((device_levels, frames, DK), f32))
        if last:
            shapes.append(pltpu.VMEM((rows, frames), f32))
        inner = pl.pallas_call(
            functools.partial(local_kernel, group, last),
            in_specs=[here] + [[here] * 2] * 2 + [here] * (8 if i else 1),
            out_specs=[here] * len(shapes),
            out_shape=shapes,
            input_output_aliases={6 + j: j for j in range(7)} if i else {},
            compiler_params=params(16),
            cost_estimate=cost(10**9, 7 * block // heads * len(group)),
        )(left, right, turned, level_weights, *(inner or []))
    q_local, k_local, v_local, _, _, _, columns, weight_grad = inner

    arrived = []
    carried = keep + partner(send, "tm", 0)
    for height in range(1, device_levels):
        other = partner(carried, "tm", height)
        arrived.append(other[0])
        carried = carried[1:] + other[1:]
    states = [partner(near, "tm", 0)]
    for height in range(far):
        states += [partner(arrived[height], "tm", 0), arrived[height]]

    def coarse(span, query, weight):
        used = states[: 2 * span.stop - 1]
        return pl.pallas_call(
            functools.partial(coarse_kernel, fine, span),
            in_specs=[here, [here] * 2] + [here] * (3 + len(used)),
            out_specs=[here] * 2,
            out_shape=[kept, pltpu.VMEM((rows, frames), f32)],
            scratch_shapes=[pltpu.VMEM((len(span), frames, DK), f32)],
            input_output_aliases={4: 0, 5: 1},
            compiler_params=params(16),
            cost_estimate=cost(10**9, 2 * block),
            name="coarse",
        )(left, right, columns, query, weight, *used)

    if far:
        q_local, weight_grad = coarse(range(far), q_local, weight_grad)
    q_local, weight_grad = coarse(range(far, device_levels), q_local, weight_grad)
    for height in range(lax.axis_size("head").bit_length() - 1):
        weight_grad = weight_grad + partner(weight_grad, "head", height)

    def back(times, operand, factor, old, extra):
        return pl.pallas_call(
            functools.partial(back_kernel, device_levels, times, operand, bool(extra)),
            in_specs=[here if operand == "left" else [here] * 2] + [here] * (1 + len(extra) + len(states)),
            out_specs=[there] * (1 + len(extra)),
            out_shape=[big] * (1 + len(extra)),
            scratch_shapes=[
                pltpu.VMEM((frames, width), f32),
                pltpu.SemaphoreType.DMA((heads + 1, frames // B)),
            ],
            compiler_params=params(16),
            cost_estimate=cost(10**9, 2 * block),
        )(factor, old, *extra, *states)

    (k_total,) = back(nt, "right", right, k_local, [])
    v_total, q_total = back(nn, "left", left, v_local, [q_local])
    return (q_total, k_total, v_total, weight_grad[:levels])


def solution(mesh):
    in_specs = (P("tm", "head"), P("tm", "head"), P("tm", "head"), P("tm", "head"), P(None, "tm"))
    out_specs = (P("tm", "head"), P("tm", "head"), P("tm", "head"), P(None, "tm"))
    return jax.shard_map(body, mesh=mesh, in_specs=in_specs, out_specs=out_specs, check_vma=False)
```

time: 54.4 us -> 51.1 us (0.939)
  the two profiles are of different devices: /device:TPU:1 before, /device:TPU:0 now
where the time goes in v1:
time: 51.1 us; the launch traced here: 50.9 us
  Pallas kernels  25.4 us (50%)
  starting transfers between devices  12.8 us (25%)
  waiting for transfers between devices  11.2 us (22%)
  between operations  0.75 us (1%)
  other arithmetic  0.7 us (1%)
    ppermute x8, starting transfers between devices, partner(): lax.ppermute(array, axis, [(i, i ^ 1 << stride) for i in range(lax.axis_s...  12.8 us
    ppermute x8, waiting for transfers between devices, partner(): lax.ppermute(array, axis, [(i, i ^ 1 << stride) for i in range(lax.axis_s...  11.2 us
    pallas_call x3, Pallas kernels, body(): pl.pallas_call(functools.partial(local_kernel, group, last), in_specs=[he...  10.7 us
    pallas_call x1, Pallas kernels, body(): pl.pallas_call(functools.partial(state_kernel, fine), in_specs=[there] *...  7.04 us
    pallas_call x2, Pallas kernels, back(): pl.pallas_call(functools.partial(back_kernel, device_levels, times, opera...  3.98 us
    pallas_call x2, Pallas kernels, coarse(): pl.pallas_call(functools.partial(coarse_kernel, fine, span), in_specs=[he...  3.67 us
  transfers between devices with their start and end apart: 8, of which 3 were waited for; matrix products, arithmetic and copies ran while one was open for 0% of the time, Pallas kernels for 33%

profile of v1, /device:TPU:0, one launch (start us, length us, event | category | flops | bytes accessed | tf_op | source)
XLA Modules:
  0.0 50.9 jit_solution(2306935162567805534)
XLA Ops:
  0.6 0.0 copy-start
  0.6 7.0 %states.1 = (f32[4,128,128]{2,1,0:T(8,128)S(1)}, f32[2,2,128,128]{3,2,1,0:T(8,128)S(1)}, f32[2,2,128,128]{3,2,1,0:T(8,128)S(1)}, bf16[2,4,1024,256]{3,2,1,0:T(8,...) custom-call(f32[1024,512]{1,0:T(8,128)} %q_hbm.1, ...), custom_call_target="tpu_custom_call" | custom-call | flops 1000000000 | bytes 8388608 | tf_op jit(solution)/shard_map/states/pallas_call | solution.py:363
  7.7 3.0 %collective-permute-start.1 = (f32[2,2,128,128]{3,2,1,0:T(8,128)S(1)}, f32[2,2,128,128]{3,2,1,0:T(8,128)S(1)}, u32[]{:S(2)}, u32[]{:S(2)}) collective-permute-start(f32[2,2,128,128]{3,2,1,0:T(8,128)S(1)} %get-tuple-element.62), channel_id=1, source_target_pairs={{0,4},{4,0},{8,12},{12,8},{16,20},{20,16},{24,28},{28,24},{1,5},{5... | collective-permute-start | bytes 786440 | tf_op jit(solution)/shard_map/ppermute | solution.py:21
  10.7 6.3 %collective-permute-done.1 = f32[2,2,128,128]{3,2,1,0:T(8,128)S(1)} collective-permute-done((f32[2,2,128,128]{3,2,1,0:T(8,128)S(1)}, f32[2,2,128,128]{3,2,1,0:T(8,128)S(1)}, u32[]{:S(2)}, u32[]{:S(2)}) %collective-permute-start.1) | collective-permute-done | bytes 262176 | tf_op jit(solution)/shard_map/ppermute | solution.py:21
  17.1 1.9 %collective-permute-start.2 = (f32[2,2,128,128]{3,2,1,0:T(8,128)S(1)}, f32[2,2,128,128]{3,2,1,0:T(8,128)S(1)}, u32[]{:S(2)}, u32[]{:S(2)}) collective-permute-start(f32[2,2,128,128]{3,2,1,0:T(8,128)S(1)} %add.12), channel_id=1, source_target_pairs={{0,8},{4,12},{8,0},{12,4},{16,24},{20,28},{24,16},{28,20},{1,9},{5... | collective-permute-start | bytes 786440 | tf_op jit(solution)/shard_map/ppermute | solution.py:21
  18.9 1.5 %collective-permute-start = (f32[4,128,128]{2,1,0:T(8,128)S(1)}, f32[4,128,128]{2,1,0:T(8,128)S(1)}, u32[]{:S(2)}, u32[]{:S(2)}) collective-permute-start(f32[4,128,128]{2,1,0:T(8,128)S(1)} %get-tuple-element.60), channel_id=1, source_target_pairs={{0,4},{4,0},{8,12},{12,8},{16,20},{20,16},{24,28},{28,24},{1,5},{5... | collective-permute-start | bytes 786440 | tf_op jit(solution)/shard_map/ppermute | solution.py:21
  20.5 4.2 %collective-permute-done.2 = f32[2,2,128,128]{3,2,1,0:T(8,128)S(1)} collective-permute-done((f32[2,2,128,128]{3,2,1,0:T(8,128)S(1)}, f32[2,2,128,128]{3,2,1,0:T(8,128)S(1)}, u32[]{:S(2)}, u32[]{:S(2)}) %collective-permute-start.2) | collective-permute-done | bytes 262176 | tf_op jit(solution)/shard_map/ppermute | solution.py:21
  24.6 2.6 %collective-permute-start.4 = (f32[1,2,128,128]{3,2,1,0:T(8,128)S(1)}, f32[1,2,128,128]{3,2,1,0:T(8,128)S(1)}, u32[]{:S(2)}, u32[]{:S(2)}) collective-permute-start(f32[1,2,128,128]{3,2,1,0:T(8,128)S(1)} %get-tuple-element.70), channel_id=1, source_target_pairs={{0,16},{4,20},{8,24},{12,28},{16,0},{20,4},{24,8},{28,12},{1,17},{... | collective-permute-start | bytes 393224 | tf_op jit(solution)/shard_map/ppermute | solution.py:21
  27.2 0.0 copy-done
  27.2 5.1 %shard_map.84 = (f32[1024,512]{1,0:T(8,128)S(1)}, f32[1024,512]{1,0:T(8,128)S(1)}, f32[1024,512]{1,0:T(8,128)S(1)}, f32[8,128,128]{2,1,0:T(8,128)S(1)}, f32[12,8...) custom-call(bf16[2,4,1024,256]{3,2,1,0:T(8,128)(2,1)S(1)} %get-tuple-element.37.left_ref.refs_0_, ...), custom_call_target="tpu_custom_call" | custom-call | flops 1000000000 | bytes 7340032 | tf_op jit(solution)/shard_map/pallas_call | solution.py:395
  32.4 1.6 %collective-permute-start.3 = (f32[2,128,128]{2,1,0:T(8,128)S(1)}, f32[2,128,128]{2,1,0:T(8,128)S(1)}, u32[]{:S(2)}, u32[]{:S(2)}) collective-permute-start(f32[2,128,128]{2,1,0:T(8,128)S(1)} %get-tuple-element.71.refs_2_.refs_5_.refs_4_), channel_id=1, source_target_pairs={{0,4},{4,0},{8,12},{12,8},{16,20},{20,16},{24,28},{28,24},{1,5},{5... | collective-permute-start | bytes 393224 | tf_op jit(solution)/shard_map/ppermute | solution.py:21
  33.9 2.7 %shard_map.85 = (f32[1024,512]{1,0:T(8,128)S(1)}, f32[1024,512]{1,0:T(8,128)S(1)}, f32[1024,512]{1,0:T(8,128)S(1)}, f32[8,128,128]{2,1,0:T(8,128)S(1)}, f32[12,8...) custom-call(bf16[2,4,1024,256]{3,2,1,0:T(8,128)(2,1)S(1)} %get-tuple, ...), custom_call_target="tpu_custom_call", output_to_operand_aliasing={{0}: (6, {}), {1}: (7, {}), {2}: (8, {}), {3}: (9, {}), {4}... | custom-call | flops 1000000000 | bytes 3670016 | tf_op jit(solution)/shard_map/pallas_call | solution.py:395
  36.6 0.0 collective-permute-done.4
  36.6 0.6 %collective-permute-start.5 = (f32[2,128,128]{2,1,0:T(8,128)S(1)}, f32[2,128,128]{2,1,0:T(8,128)S(1)}, u32[]{:S(2)}, u32[]{:S(2)}) collective-permute-start(f32[2,128,128]{2,1,0:T(8,128)S(1)} %bitcast.3), channel_id=1, source_target_pairs={{0,4},{4,0},{8,12},{12,8},{16,20},{20,16},{24,28},{28,24},{1,5},{5... | collective-permute-start | bytes 393224 | tf_op jit(solution)/shard_map/ppermute | solution.py:21
  37.2 2.9 %shard_map.86 = (f32[1024,512]{1,0:T(8,128)S(1)}, f32[1024,512]{1,0:T(8,128)S(1)}, f32[1024,512]{1,0:T(8,128)S(1)}, f32[8,128,128]{2,1,0:T(8,128)S(1)}, f32[12,8...) custom-call(bf16[2,4,1024,256]{3,2,1,0:T(8,128)(2,1)S(1)} %get-tuple, ...), custom_call_target="tpu_custom_call", output_to_operand_aliasing={{0}: (6, {}), {1}: (7, {}), {2}: (8, {}), {3}: (9, {}), {4}... | custom-call | flops 1000000000 | bytes 3670016 | tf_op jit(solution)/shard_map/pallas_call | solution.py:395
  40.1 0.0 collective-permute-done.refs_0_.refs_3_.refs_2_
  40.1 0.0 collective-permute-done.3.refs_1_.refs_4_.refs_3_
  40.1 2.3 %coarse.2 = (f32[1024,512]{1,0:T(8,128)S(1)}, f32[16,1024]{1,0:T(8,128)S(1)}) custom-call(bf16[2,4,1024,256]{3,2,1,0:T(8,128)(2,1)S(1)} %get-tuple-element.37.left_ref.refs_0_, bf16[2,2,1024,256]{3,2,1,0:T(8,128)(2,1)S(1)} %get-tuple-element.38.right_refs_0_.refs_0__0_, ...), custom_call_target="tpu_custom_call", output_to_operand_aliasing={{0}: (4, {}), {1}: (5, {})} | custom-call | flops 1000000000 | bytes 4194304 | tf_op jit(solution)/shard_map/coarse/pallas_call | solution.py:418
  42.5 0.0 collective-permute-done.5.refs_3_.refs_6_.refs_5_
  42.5 1.3 %coarse.3 = (f32[1024,512]{1,0:T(8,128)S(1)}, f32[16,1024]{1,0:T(8,128)S(1)}) custom-call(bf16[2,4,1024,256]{3,2,1,0:T(8,128)(2,1)S(1)} %get-tuple-element.37.left_ref.refs_0_, bf16[2,2,1024,256]{3,2,1,0:T(8,128)(2,1)S(1)} %get-tuple-element.38.right_refs_0_.refs_0__0_, ...), custom_call_target="tpu_custom_call", output_to_operand_aliasing={{0}: (4, {}), {1}: (5, {})} | custom-call | flops 1000000000 | bytes 4194304 | tf_op jit(solution)/shard_map/coarse/pallas_call | solution.py:418
  43.8 0.1 collective-permute-start.6
  43.9 1.8 %shard_map.88 = f32[1024,512]{1,0:T(8,128)} custom-call(bf16[2,2,1024,256]{3,2,1,0:T(8,128)(2,1)S(1)} %get-tuple-element.38.right_refs_0_.refs_0__0_, bf16[2,2,1024,256]{3,2,1,0:T(8,128)(2,1)S(1)} %get-tuple-element.39.right_refs_1_.refs_0__1_, f32[1024,512]{1,0:T(8,128)S(1)} %get-tuple-element.67.refs_1_, ...), custom_call_target="tpu_custom_call" | custom-call | flops 1000000000 | bytes 4194304 | tf_op jit(solution)/shard_map/pallas_call | solution.py:437
  45.7 0.0 collective-permute-done.6
  45.7 1.6 %collective-permute-start.7 = (f32[16,1024]{1,0:T(8,128)S(1)}, f32[16,1024]{1,0:T(8,128)S(1)}, u32[]{:S(2)}, u32[]{:S(2)}) collective-permute-start(f32[16,1024]{1,0:T(8,128)S(1)} %add.14), channel_id=1, source_target_pairs={{0,2},{1,3},{2,0},{3,1},{4,6},{5,7},{6,4},{7,5},{8,10},{9,11},{10,... | collective-permute-start | bytes 196616 | tf_op jit(solution)/shard_map/ppermute | solution.py:21
  47.3 2.2 %shard_map.87 = (f32[1024,512]{1,0:T(8,128)}, f32[1024,512]{1,0:T(8,128)}) custom-call(bf16[2,4,1024,256]{3,2,1,0:T(8,128)(2,1)S(1)} %get-tuple-element.37.left_ref.refs_0_, f32[1024,512]{1,0:T(8,128)S(1)} %get-tuple-element.56.refs_1_, f32[1024,512]{1,0:T(8,128)S(1)} %get-tuple-element.65.refs_2_, ...), custom_call_target="tpu_custom_call" | custom-call | flops 1000000000 | bytes 4194304 | tf_op jit(solution)/shard_map/pallas_call | solution.py:437
  49.5 0.8 %collective-permute-done.7 = f32[16,1024]{1,0:T(8,128)S(1)} collective-permute-done((f32[16,1024]{1,0:T(8,128)S(1)}, f32[16,1024]{1,0:T(8,128)S(1)}, u32[]{:S(2)}, u32[]{:S(2)}) %collective-permute-start.7) | collective-permute-done | bytes 65568 | tf_op jit(solution)/shard_map/ppermute | solution.py:21
  50.3 0.6 %slice_add_fusion.1 = f32[14,1024]{1,0:T(8,128)} fusion(f32[16,1024]{1,0:T(8,128)S(1)} %collective-permute-done.7, f32[16,1024]{1,0:T(8,128)S(1)} %add.14), kind=kLoop, calls=%fused_computation.2 | loop fusion | flops 14336 | bytes 172032 | tf_op jit(solution)/shard_map/add | solution.py:434
  (3 shorter events, 0.1 us)
Async XLA Ops:
  0.6 26.6 %copy-start = (f32[14,1024]{1,0:T(8,128)S(1)}, f32[14,1024]{1,0:T(8,128)}, u32[]{:S(2)}) copy-start(f32[14,1024]{1,0:T(8,128)} %w_ref.5) | copy-start | bytes 172036
  7.7 9.3 %collective-permute-start.1 = (f32[2,2,128,128]{3,2,1,0:T(8,128)S(1)}, f32[2,2,128,128]{3,2,1,0:T(8,128)S(1)}, u32[]{:S(2)}, u32[]{:S(2)}) collective-permute-start(f32[2,2,128,128]{3,2,1,0:T(8,128)S(1)} %get-tuple-element.62), channel_id=1, source_target_pairs={{0,4},{4,0},{8,12},{12,8},{16,20},{20,16},{24,28},{28,24},{1,5},{5... | collective-permute-start | bytes 786440 | tf_op jit(solution)/shard_map/ppermute | solution.py:21
  17.1 7.5 %collective-permute-start.2 = (f32[2,2,128,128]{3,2,1,0:T(8,128)S(1)}, f32[2,2,128,128]{3,2,1,0:T(8,128)S(1)}, u32[]{:S(2)}, u32[]{:S(2)}) collective-permute-start(f32[2,2,128,128]{3,2,1,0:T(8,128)S(1)} %add.12), channel_id=1, source_target_pairs={{0,8},{4,12},{8,0},{12,4},{16,24},{20,28},{24,16},{28,20},{1,9},{5... | collective-permute-start | bytes 786440 | tf_op jit(solution)/shard_map/ppermute | solution.py:21
  18.9 21.2 %collective-permute-start = (f32[4,128,128]{2,1,0:T(8,128)S(1)}, f32[4,128,128]{2,1,0:T(8,128)S(1)}, u32[]{:S(2)}, u32[]{:S(2)}) collective-permute-start(f32[4,128,128]{2,1,0:T(8,128)S(1)} %get-tuple-element.60), channel_id=1, source_target_pairs={{0,4},{4,0},{8,12},{12,8},{16,20},{20,16},{24,28},{28,24},{1,5},{5... | collective-permute-start | bytes 786440 | tf_op jit(solution)/shard_map/ppermute | solution.py:21
  24.6 12.0 %collective-permute-start.4 = (f32[1,2,128,128]{3,2,1,0:T(8,128)S(1)}, f32[1,2,128,128]{3,2,1,0:T(8,128)S(1)}, u32[]{:S(2)}, u32[]{:S(2)}) collective-permute-start(f32[1,2,128,128]{3,2,1,0:T(8,128)S(1)} %get-tuple-element.70), channel_id=1, source_target_pairs={{0,16},{4,20},{8,24},{12,28},{16,0},{20,4},{24,8},{28,12},{1,17},{... | collective-permute-start | bytes 393224 | tf_op jit(solution)/shard_map/ppermute | solution.py:21
  32.4 7.7 %collective-permute-start.3 = (f32[2,128,128]{2,1,0:T(8,128)S(1)}, f32[2,128,128]{2,1,0:T(8,128)S(1)}, u32[]{:S(2)}, u32[]{:S(2)}) collective-permute-start(f32[2,128,128]{2,1,0:T(8,128)S(1)} %get-tuple-element.71.refs_2_.refs_5_.refs_4_), channel_id=1, source_target_pairs={{0,4},{4,0},{8,12},{12,8},{16,20},{20,16},{24,28},{28,24},{1,5},{5... | collective-permute-start | bytes 393224 | tf_op jit(solution)/shard_map/ppermute | solution.py:21
  36.6 5.9 %collective-permute-start.5 = (f32[2,128,128]{2,1,0:T(8,128)S(1)}, f32[2,128,128]{2,1,0:T(8,128)S(1)}, u32[]{:S(2)}, u32[]{:S(2)}) collective-permute-start(f32[2,128,128]{2,1,0:T(8,128)S(1)} %bitcast.3), channel_id=1, source_target_pairs={{0,4},{4,0},{8,12},{12,8},{16,20},{20,16},{24,28},{28,24},{1,5},{5... | collective-permute-start | bytes 393224 | tf_op jit(solution)/shard_map/ppermute | solution.py:21
  43.8 1.9 %collective-permute-start.6 = (f32[16,1024]{1,0:T(8,128)S(1)}, f32[16,1024]{1,0:T(8,128)S(1)}, u32[]{:S(2)}, u32[]{:S(2)}) collective-permute-start(f32[16,1024]{1,0:T(8,128)S(1)} %get-tuple-element.69), channel_id=1, source_target_pairs={{0,1},{1,0},{2,3},{3,2},{4,5},{5,4},{6,7},{7,6},{8,9},{9,8},{10,11... | collective-permute-start | bytes 196616 | tf_op jit(solution)/shard_map/ppermute | solution.py:21
  45.7 4.5 %collective-permute-start.7 = (f32[16,1024]{1,0:T(8,128)S(1)}, f32[16,1024]{1,0:T(8,128)S(1)}, u32[]{:S(2)}, u32[]{:S(2)}) collective-permute-start(f32[16,1024]{1,0:T(8,128)S(1)} %add.14), channel_id=1, source_target_pairs={{0,2},{1,3},{2,0},{3,1},{4,6},{5,7},{6,4},{7,5},{8,10},{9,11},{10,... | collective-permute-start | bytes 196616 | tf_op jit(solution)/shard_map/ppermute | solution.py:21

commit v2 on v1

v2 whole, which is shorter than its diff:
```python
import functools

import jax
import jax.numpy as jnp
from jax import lax
from jax.experimental import pallas as pl
from jax.experimental.pallas import tpu as pltpu
from jax.sharding import PartitionSpec as P


DK = 128
C = 128
B = 256
SUB = 8
NN = (((1,), (0,)), ((), ()))
NT = (((1,), (1,)), ((), ()))
TN = (((0,), (0,)), ((), ()))


def partner(array, axis, stride):
    return lax.ppermute(array, axis, [(i, i ^ 1 << stride) for i in range(lax.axis_size(axis))])


def split(x):
    hi = x.astype(jnp.bfloat16)
    return hi, (x - hi.astype(jnp.float32)).astype(jnp.bfloat16)


def wide(parts):
    return jnp.concatenate(parts, axis=1)


def tall(parts):
    return jnp.concatenate(parts, axis=0)


def dot(a, b, dims):
    return lax.dot_general(a, b, dims, preferred_element_type=jnp.float32)


def halves(x):
    n = x.shape[1] // 2
    return x[:, :n] + x[:, n:]


def nn(a, b):
    right = wide(b)
    return halves(dot(wide(a), tall((right, right)), NN))


def nt(a, b):
    return halves(dot(wide(a), tall((wide((b[0], b[0])), wide((b[1], b[1])))), NT))


def tn(a, b):
    right = wide(b)
    return halves(dot(tall(a), tall((right, right)), TN))


def fold(x):
    return jnp.sum(x.reshape(x.shape[0] // SUB, SUB, x.shape[1]), axis=0)


def level_table():
    s = lax.broadcasted_iota(jnp.int32, (C, C), 0)
    t = lax.broadcasted_iota(jnp.int32, (C, C), 1)
    x = jnp.bitwise_xor(s, t)
    level = jnp.zeros((C, C), jnp.int32)
    for height in range(C.bit_length() - 1):
        level = level + (x >= 1 << height).astype(jnp.int32)
    return jnp.where(s <= t, level, -1)


def bit_of(level):
    return jnp.bitwise_and(jnp.right_shift(lax.axis_index("tm"), level), 1)


def halving_bit(level):
    return min(level, 2) - 1


def product(bit, row, turned, rights):
    grown = wide(split(jnp.where(bit == 1, row * turned[1], turned[0])))
    right = jnp.where(bit == 1, rights[1], rights[0])
    return dot(grown, tall((right, right)), NN)


def state_kernel(first, levels, k_hbm, q_hbm, v_hbm, d_hbm, w_hbm, send_refs, keep_refs, kq_ref, right_ref, turned_ref, w_ref, stage_ref, sum_ref, sems, w_sem):
    heads, frames = kq_ref.shape[1:3]
    half = heads // 2

    def copies(head):
        lanes = pl.ds(head * DK, DK)
        ends = (kq_ref.at[0, head], kq_ref.at[1, head], stage_ref.at[0, head], stage_ref.at[1, head])
        return [
            pltpu.make_async_copy(x.at[:, lanes], end, sems.at[i, head])
            for i, (x, end) in enumerate(zip((k_hbm, q_hbm, v_hbm, d_hbm), ends))
        ]

    def start(head):
        if head < heads:
            for copy in copies(head):
                copy.start()

    weights = pltpu.make_async_copy(w_hbm, w_ref, w_sem)
    weights.start()
    start(0)
    start(1)
    weights.wait()
    for head in range(heads):
        for copy in copies(head):
            copy.wait()
        start(head + 2)
        for b in range(frames // B):
            span = slice(b * B, (b + 1) * B)
            turned, rights = [], []
            for i in range(2):
                turned.append(kq_ref[i, head, span, :].T)
                rights.append(wide(split(stage_ref[i, head, span, :])))
                turned_ref[i, head, :, span] = turned[i]
                right_ref[i, head, span, :] = rights[i]
            for level in range(1, levels):
                row = w_ref[first + level : first + level + 1, span]
                term = product(bit_of(level), row, turned, rights)
                sum_ref[head, level - 1] = sum_ref[head, level - 1] + term if b else term
    for level in range(1, levels):
        own = bit_of(halving_bit(level))
        for j in range(half):
            low, high = halves(sum_ref[j, level - 1]), halves(sum_ref[half + j, level - 1])
            send_refs[level - 1][j] = jnp.where(own == 0, high, low)
            keep_refs[level - 1][j] = jnp.where(own == 0, low, high)


def near_kernel(first, right_ref, turned_ref, w_ref, near_ref):
    heads, frames = right_ref.shape[1:3]
    for head in range(heads):
        total = None
        for b in range(frames // B):
            span = slice(b * B, (b + 1) * B)
            turned = [turned_ref[i, head, :, span] for i in range(2)]
            rights = [right_ref[i, head, span, :] for i in range(2)]
            term = product(bit_of(0), w_ref[first : first + 1, span], turned, rights)
            total = term if total is None else total + term
        near_ref[head] = halves(total)


def upper_pairs(chunks):
    heights = chunks.bit_length() - 1
    return [(c, k) for c in range(chunks) for k in range(heights) if c >> k & 1]


def parts(ref, *at):
    x = ref[at]
    return x[:, :DK], x[:, DK:]


def local_kernel(heads, last, kq_ref, right_ref, turned_ref, w_ref, *refs):
    start = heads[0] == 0
    if not start:
        refs = refs[7:]
    qg_ref, kg_ref, vg_ref, pr_ref, wc_ref, mix_ref, col_ref = refs[:7]
    left_ref = refs[-1]
    frames = kq_ref.shape[2]
    chunks = frames // C
    heights = chunks.bit_length() - 1
    inner = C.bit_length()
    pairs = upper_pairs(chunks)
    spans = [slice(c * C, (c + 1) * C) for c in range(chunks)]

    if start:
        table = level_table()
        for c in range(chunks):
            mixing = jnp.zeros((C, C), jnp.float32)
            for level in range(inner):
                mixing = jnp.where(table == level, w_ref[level : level + 1, spans[c]], mixing)
            mix_ref[c] = mixing
            for i in range(col_ref.shape[0]):
                level = inner + heights + i
                col_ref[i, spans[c], :] = jnp.broadcast_to(w_ref[level : level + 1, spans[c]], (C, C)).T

    def right(i, head, span):
        return parts(right_ref, i, head, span)

    def add(head, ref, at, value):
        ref[at] = ref[at] + value if head else value

    def inside(head):
        lanes = slice(head * DK, (head + 1) * DK)
        sums, back = {}, {}
        place = head - heads[0]
        for c in range(chunks):
            for i in range(2):
                left_ref[place, i, spans[c], :] = wide(split(kq_ref[i, head, spans[c], :]))
        for c in range(chunks - 1):
            sums[c, 0] = tn(parts(left_ref, place, 0, spans[c]), right(0, head, spans[c]))
        for k in range(1, heights):
            for b in range(chunks >> k):
                if b << k < chunks - (1 << k):
                    sums[b, k] = sums[2 * b, k - 1] + sums[2 * b + 1, k - 1]

        def scores(c):
            ks, qs = parts(left_ref, place, 0, spans[c]), parts(left_ref, place, 1, spans[c])
            vs, ds = right(0, head, spans[c]), right(1, head, spans[c])
            gt = nt(ks, qs)
            et = nt(vs, ds)
            add(head, pr_ref, c, gt * et)
            mt = mix_ref[c]
            return split(mt * et), split(mt * gt)

        def gradients(c, me, mg):
            ks, qs = parts(left_ref, place, 0, spans[c]), parts(left_ref, place, 1, spans[c])
            vs, ds = right(0, head, spans[c]), right(1, head, spans[c])
            kg, vg, qg = nn(me, qs), nn(mg, ds), tn(me, ks)
            if c < chunks - 1:
                total = None
                for k in range(heights):
                    if not c >> k & 1:
                        term = back[c >> k, k]
                        total = term if total is None else total + term
                bs = split(total)
                kg = kg + nt(vs, bs)
                vg = vg + nn(ks, bs)
            kg_ref[spans[c], lanes] = kg
            vg_ref[spans[c], lanes] = vg
            ups = [k for k in range(heights) if c >> k & 1]
            if ups:
                qt = turned_ref[1, head, :, spans[c]]
                mixed = None
                for k in ups:
                    row = w_ref[inner + k : inner + k + 1, spans[c]]
                    along = nt(split(sums[(c >> k) - 1, k]), ds)
                    add(head, wc_ref, pairs.index((c, k)), fold(qt * along))
                    term = row * along
                    mixed = term if mixed is None else mixed + term
                    grad = nn(split(row * qt), ds)
                    key = ((c >> k) - 1, k)
                    back[key] = back[key] + grad if key in back else grad
                qg = qg + mixed.T
            qg_ref[spans[c], lanes] = qg

        waiting = None
        for c in reversed(range(chunks)):
            now = scores(c)
            if waiting is not None:
                gradients(c + 1, *waiting)
            waiting = now
        gradients(0, *waiting)

    for head in heads:
        inside(head)

    if last:
        wg_ref = refs[7]
        table = level_table()
        wg_ref[...] = jnp.zeros_like(wg_ref)
        for c in range(chunks):
            product = pr_ref[c]
            for level in range(inner):
                row = jnp.sum(jnp.where(table == level, product, 0.0), axis=0, keepdims=True)
                wg_ref[level : level + 1, spans[c]] = row
        for i, (c, k) in enumerate(pairs):
            wg_ref[inner + k : inner + k + 1, spans[c]] = jnp.sum(wc_ref[i], axis=0, keepdims=True)


def received(level, head, half, refs):
    if level == 0:
        return refs[0][head]
    other, mine = refs[2 * level - 1], refs[2 * level]
    return jnp.where(bit_of(halving_bit(level)) == head // half, mine[head % half], other[head % half])


def coarse_kernel(first, levels, kq_ref, right_ref, col_ref, old_q, old_w, *refs):
    arrived, (out_ref, wg_ref, product_ref) = refs[:-3], refs[-3:]
    heads, frames = kq_ref.shape[1:3]
    arrived = [None] * (2 * levels[-1] + 1 - len(arrived)) + list(arrived)
    for head in range(heads):
        lanes = slice(head * DK, (head + 1) * DK)
        states = []
        for level in levels:
            state = received(level, head, heads // 2, arrived)
            states.append(split(jnp.where(bit_of(level) == 1, state, 0.0)))
        for b in range(frames // B):
            span = slice(b * B, (b + 1) * B)
            ds = parts(right_ref, 1, head, span)
            q = kq_ref[1, head, span, :]
            mixed = old_q[span, lanes]
            for i, level in enumerate(levels):
                along = nt(ds, states[i])
                product_ref[i, span, :] = product_ref[i, span, :] + q * along if head else q * along
                mixed = mixed + col_ref[level, span, :] * along
            out_ref[span, lanes] = mixed
    for i, level in enumerate(levels):
        for c in range(frames // C):
            span = slice(c * C, (c + 1) * C)
            row = jnp.sum(product_ref[i, span, :].T, axis=0, keepdims=True)
            wg_ref[first + level : first + level + 1, span] = row


def back_kernel(levels, kq_ref, right_ref, old_k, old_v, q_ref, *refs):
    arrived = refs[: 2 * levels - 1]
    k_hbm, v_hbm, q_hbm, k_ref, v_ref, sems, q_sem = refs[2 * levels - 1 :]
    heads, frames = kq_ref.shape[1:3]
    blocks = frames // B
    queries = pltpu.make_async_copy(q_ref, q_hbm, q_sem)
    queries.start()

    def copies(head, b):
        at = (slice(b * B, (b + 1) * B), slice(head * DK, (head + 1) * DK))
        return [
            pltpu.make_async_copy(x.at[at], end.at[at], sems.at[i, head, b])
            for i, (x, end) in enumerate(((k_ref, k_hbm), (v_ref, v_hbm)))
        ]

    for head in range(heads):
        lanes = slice(head * DK, (head + 1) * DK)
        total = None
        for level in range(levels):
            state = received(level, head, heads // 2, arrived)
            term = jnp.where(bit_of(level) == 0, state, 0.0)
            total = term if total is None else total + term
        bs = split(total)
        for b in range(blocks):
            span = slice(b * B, (b + 1) * B)
            k_ref[span, lanes] = old_k[span, lanes] + nt(parts(right_ref, 0, head, span), bs)
            v_ref[span, lanes] = old_v[span, lanes] + nn(split(kq_ref[0, head, span, :]), bs)
            for copy in copies(head, b):
                copy.start()
    for head in range(heads):
        for b in range(blocks):
            for copy in copies(head, b):
                copy.wait()
    queries.wait()


def params(mib):
    return pltpu.CompilerParams(vmem_limit_bytes=mib * 2**20)


def cost(flops, size):
    return pl.CostEstimate(flops=flops, bytes_accessed=size, transcendentals=0)


def body(query_rows, key_rows, value_rows, out_grad, level_weights):
    frames, width = query_rows.shape
    heads = width // DK
    half = heads // 2
    levels = level_weights.shape[0]
    fine = frames.bit_length()
    device_levels = levels - fine
    far = device_levels - 1
    f32, bf16 = jnp.float32, jnp.bfloat16
    big = jax.ShapeDtypeStruct((frames, width), f32)
    kept = pltpu.VMEM((frames, width), f32)
    chunks = frames // C
    pairs = max(1, len(upper_pairs(chunks)))
    block = frames * width * 4
    here = pl.BlockSpec(memory_space=pltpu.VMEM)
    there = pl.BlockSpec(memory_space=pl.ANY)
    inputs = [pltpu.with_memory_space_constraint(x, pltpu.HBM) for x in (query_rows, key_rows, value_rows, out_grad, level_weights)]
    part = jax.ShapeDtypeStruct((half, DK, DK), f32)
    rows = -(-levels // SUB) * SUB

    send, keep, kq, right, turned = pl.pallas_call(
        functools.partial(state_kernel, fine, device_levels),
        in_specs=[there] * 5,
        out_specs=[[here] * far] * 2 + [here] * 3,
        out_shape=[
            [part] * far,
            [part] * far,
            pltpu.VMEM((2, heads, frames, DK), f32),
            pltpu.VMEM((2, heads, frames, 2 * DK), bf16),
            pltpu.VMEM((2, heads, DK, frames), f32),
        ],
        scratch_shapes=[
            pltpu.VMEM((levels, frames), f32),
            pltpu.VMEM((2, heads, frames, DK), f32),
            pltpu.VMEM((heads, far, DK, 2 * DK), f32),
            pltpu.SemaphoreType.DMA((4, heads)),
            pltpu.SemaphoreType.DMA,
        ],
        compiler_params=params(16),
        cost_estimate=cost(10**9, 4 * block),
        name="states",
    )(inputs[1], inputs[0], *inputs[2:])

    near = pl.pallas_call(
        functools.partial(near_kernel, fine),
        in_specs=[here] * 3,
        out_specs=here,
        out_shape=jax.ShapeDtypeStruct((heads, DK, DK), f32),
        compiler_params=params(16),
        cost_estimate=cost(10**9, block),
        name="near",
    )(right, turned, level_weights)

    inner = None
    for head in range(heads):
        last = head == heads - 1
        shapes = [kept] * 3
        shapes += [pltpu.VMEM((chunks, C, C), f32), pltpu.VMEM((pairs, SUB, C), f32), pltpu.VMEM((chunks, C, C), f32)]
        shapes.append(pltpu.VMEM((device_levels, frames, DK), f32))
        if last:
            shapes.append(pltpu.VMEM((rows, frames), f32))
        inner = pl.pallas_call(
            functools.partial(local_kernel, [head], last),
            in_specs=[here] * (11 if head else 4),
            out_specs=[here] * len(shapes),
            out_shape=shapes,
            scratch_shapes=[pltpu.VMEM((1, 2, frames, 2 * DK), bf16)],
            input_output_aliases={4 + j: j for j in range(7)} if head else {},
            compiler_params=params(16),
            cost_estimate=cost(10**9, 7 * block // heads),
        )(kq, right, turned, level_weights, *(inner or []))
    q_local, k_local, v_local, _, _, _, columns, weight_grad = inner

    states = [partner(near, "tm", 0)]
    for level in range(1, device_levels):
        halver = halving_bit(level)
        carried = keep[level - 1] + partner(send[level - 1], "tm", halver)
        for height in range(level):
            if height != halver:
                carried = carried + partner(carried, "tm", height)
        carried = partner(carried, "tm", level)
        states += [partner(carried, "tm", halver), carried]

    def coarse(span, query, weight):
        used = states[max(0, 2 * span[0] - 1) : 2 * span[-1] + 1]
        return pl.pallas_call(
            functools.partial(coarse_kernel, fine, span),
            in_specs=[here] * (5 + len(used)),
            out_specs=[here] * 2,
            out_shape=[kept, pltpu.VMEM((rows, frames), f32)],
            scratch_shapes=[pltpu.VMEM((len(span), frames, DK), f32)],
            input_output_aliases={3: 0, 4: 1},
            compiler_params=params(16),
            cost_estimate=cost(10**9, 2 * block),
            name="coarse",
        )(kq, right, columns, query, weight, *used)

    q_local, weight_grad = coarse(list(range(far)), q_local, weight_grad)
    q_local, weight_grad = coarse([far], q_local, weight_grad)
    for height in range(lax.axis_size("head").bit_length() - 1):
        weight_grad = weight_grad + partner(weight_grad, "head", height)

    k_total, v_total, q_total = pl.pallas_call(
        functools.partial(back_kernel, device_levels),
        in_specs=[here] * (5 + len(states)),
        out_specs=[there] * 3,
        out_shape=[big] * 3,
        scratch_shapes=[
            pltpu.VMEM((frames, width), f32),
            pltpu.VMEM((frames, width), f32),
            pltpu.SemaphoreType.DMA((2, heads, frames // B)),
            pltpu.SemaphoreType.DMA,
        ],
        compiler_params=params(16),
        cost_estimate=cost(10**9, 4 * block),
        name="back",
    )(kq, right, k_local, v_local, q_local, *states)
    return (q_total, k_total, v_total, weight_grad[:levels])


def solution(mesh):
    in_specs = (P("tm", "head"), P("tm", "head"), P("tm", "head"), P("tm", "head"), P(None, "tm"))
    out_specs = (P("tm", "head"), P("tm", "head"), P("tm", "head"), P(None, "tm"))
    return jax.shard_map(body, mesh=mesh, in_specs=in_specs, out_specs=out_specs, check_vma=False)
```

time: 51.1 us -> 44 us (0.86)
  the two profiles are of different devices: /device:TPU:0 before, /device:TPU:1 now
where the time goes in v2:
time: 44 us; the launch traced here: 43.2 us
  Pallas kernels  24 us (55%)
  starting transfers between devices  14.8 us (34%)
  waiting for transfers between devices  2.91 us (7%)
  between operations  0.77 us (2%)
  other arithmetic  0.7 us (2%)
    ppermute x10, starting transfers between devices, partner(): lax.ppermute(array, axis, [(i, i ^ 1 << stride) for i in range(lax.axis_s...  14.8 us
    pallas_call x4, Pallas kernels, body(): pl.pallas_call(functools.partial(local_kernel, [head], last), in_specs=[h...  11 us
    pallas_call x1, Pallas kernels, body(): pl.pallas_call(functools.partial(state_kernel, fine, device_levels), in_s...  5.35 us
    pallas_call x2, Pallas kernels, coarse(): pl.pallas_call(functools.partial(coarse_kernel, fine, span), in_specs=[he...  3.63 us
    pallas_call x1, Pallas kernels, body(): pl.pallas_call(functools.partial(back_kernel, device_levels), in_specs=[h...  3.18 us
    ppermute x10, waiting for transfers between devices, partner(): lax.ppermute(array, axis, [(i, i ^ 1 << stride) for i in range(lax.axis_s...  2.91 us
  transfers between devices with their start and end apart: 10, of which 2 were waited for; matrix products, arithmetic and copies ran while one was open for 0% of the time, Pallas kernels for 40%

profile of v2, /device:TPU:1, one launch (start us, length us, event | category | flops | bytes accessed | tf_op | source)
XLA Modules:
  0.0 43.2 jit_solution(15412443314433665256)
XLA Ops:
  0.6 0.0 copy-start
  0.6 5.3 %states.1 = (f32[2,128,128]{2,1,0:T(8,128)S(1)}, f32[2,128,128]{2,1,0:T(8,128)S(1)}, f32[2,128,128]{2,1,0:T(8,128)S(1)}, f32[2,128,128]{2,1,0:T(8,128)S(1)}, f32...) custom-call(f32[1024,512]{1,0:T(8,128)} %k_hbm.1, ...), custom_call_target="tpu_custom_call" | custom-call | flops 1000000000 | bytes 8388608 | tf_op jit(solution)/shard_map/states/pallas_call | solution.py:363
  6.0 2.2 %collective-permute-start.4 = (f32[2,128,128]{2,1,0:T(8,128)S(1)}, f32[2,128,128]{2,1,0:T(8,128)S(1)}, u32[]{:S(2)}, u32[]{:S(2)}) collective-permute-start(f32[2,128,128]{2,1,0:T(8,128)S(1)} %get-tuple-element.78), channel_id=1, source_target_pairs={{0,8},{4,12},{8,0},{12,4},{16,24},{20,28},{24,16},{28,20},{1,9},{5... | collective-permute-start | bytes 393224 | tf_op jit(solution)/shard_map/ppermute | solution.py:21
  8.2 1.2 %collective-permute-start.1 = (f32[2,128,128]{2,1,0:T(8,128)S(1)}, f32[2,128,128]{2,1,0:T(8,128)S(1)}, u32[]{:S(2)}, u32[]{:S(2)}) collective-permute-start(f32[2,128,128]{2,1,0:T(8,128)S(1)} %get-tuple-element.74), channel_id=1, source_target_pairs={{0,4},{4,0},{8,12},{12,8},{16,20},{20,16},{24,28},{28,24},{1,5},{5... | collective-permute-start | bytes 393224 | tf_op jit(solution)/shard_map/ppermute | solution.py:21
  9.4 2.0 %collective-permute-done.4 = f32[2,128,128]{2,1,0:T(8,128)S(1)} collective-permute-done((f32[2,128,128]{2,1,0:T(8,128)S(1)}, f32[2,128,128]{2,1,0:T(8,128)S(1)}, u32[]{:S(2)}, u32[]{:S(2)}) %collective-permute-start.4) | collective-permute-done | bytes 131104 | tf_op jit(solution)/shard_map/ppermute | solution.py:21
  11.4 1.2 %collective-permute-start.5 = (f32[2,128,128]{2,1,0:T(8,128)S(1)}, f32[2,128,128]{2,1,0:T(8,128)S(1)}, u32[]{:S(2)}, u32[]{:S(2)}) collective-permute-start(f32[2,128,128]{2,1,0:T(8,128)S(1)} %add.16), channel_id=1, source_target_pairs={{0,4},{4,0},{8,12},{12,8},{16,20},{20,16},{24,28},{28,24},{1,5},{5... | collective-permute-start | bytes 393224 | tf_op jit(solution)/shard_map/ppermute | solution.py:21
  12.6 0.0 copy-done
  12.6 0.8 %near.1 = f32[4,128,128]{2,1,0:T(8,128)S(1)} custom-call(bf16[2,4,1024,256]{3,2,1,0:T(8,128)(2,1)S(1)} %get-tuple-element.45.right_ref, f32[2,4,128,1024]{3,2,1,0:T(8,128)S(1)} %get-tuple-element.46.turned_ref, f32[14,1024]{1,0:T(8,128)S(1)} %copy-done), custom_call_target="tpu_custom_call" | custom-call | flops 1000000000 | bytes 2097152 | tf_op jit(solution)/shard_map/near/pallas_call | solution.py:386
  13.4 0.4 collective-permute-start
  13.8 0.0 collective-permute-done.1
  13.9 1.3 %collective-permute-start.2 = (f32[2,128,128]{2,1,0:T(8,128)S(1)}, f32[2,128,128]{2,1,0:T(8,128)S(1)}, u32[]{:S(2)}, u32[]{:S(2)}) collective-permute-start(f32[2,128,128]{2,1,0:T(8,128)S(1)} %add.15), channel_id=1, source_target_pairs={{0,8},{4,12},{8,0},{12,4},{16,24},{20,28},{24,16},{28,20},{1,9},{5... | collective-permute-start | bytes 393224 | tf_op jit(solution)/shard_map/ppermute | solution.py:21
  15.1 2.7 %shard_map.84 = (f32[1024,512]{1,0:T(8,128)S(1)}, f32[1024,512]{1,0:T(8,128)S(1)}, f32[1024,512]{1,0:T(8,128)S(1)}, f32[8,128,128]{2,1,0:T(8,128)S(1)}, f32[12,8...) custom-call(f32[2,4,1024,128]{3,2,1,0:T(8,128)S(1)} %get-tuple-element.44.kq_ref, ...), custom_call_target="tpu_custom_call" | custom-call | flops 1000000000 | bytes 3670016 | tf_op jit(solution)/shard_map/pallas_call | solution.py:404
  17.8 0.0 collective-permute-done.5
  17.9 2.4 %collective-permute-start.6 = (f32[2,128,128]{2,1,0:T(8,128)S(1)}, f32[2,128,128]{2,1,0:T(8,128)S(1)}, u32[]{:S(2)}, u32[]{:S(2)}) collective-permute-start(f32[2,128,128]{2,1,0:T(8,128)S(1)} %add.17), channel_id=1, source_target_pairs={{0,16},{4,20},{8,24},{12,28},{16,0},{20,4},{24,8},{28,12},{1,17},{... | collective-permute-start | bytes 393224 | tf_op jit(solution)/shard_map/ppermute | solution.py:21
  20.3 2.7 %shard_map.85 = (f32[1024,512]{1,0:T(8,128)S(1)}, f32[1024,512]{1,0:T(8,128)S(1)}, f32[1024,512]{1,0:T(8,128)S(1)}, f32[8,128,128]{2,1,0:T(8,128)S(1)}, f32[12,8...) custom-call(f32[2,4,1024,128]{3,2,1,0:T(8,128)S(1)} %get-tuple-eleme, ...), custom_call_target="tpu_custom_call", output_to_operand_aliasing={{0}: (4, {}), {1}: (5, {}), {2}: (6, {}), {3}: (7, {}), {4}... | custom-call | flops 1000000000 | bytes 3670016 | tf_op jit(solution)/shard_map/pallas_call | solution.py:404
  22.9 0.0 collective-permute-done.2.refs_2_
  23.0 1.3 %collective-permute-start.3 = (f32[2,128,128]{2,1,0:T(8,128)S(1)}, f32[2,128,128]{2,1,0:T(8,128)S(1)}, u32[]{:S(2)}, u32[]{:S(2)}) collective-permute-start(f32[2,128,128]{2,1,0:T(8,128)S(1)} %collective-permute-done.2.refs_2_), channel_id=1, source_target_pairs={{0,4},{4,0},{8,12},{12,8},{16,20},{20,16},{24,28},{28,24},{1,5},{5... | collective-permute-start | bytes 393224 | tf_op jit(solution)/shard_map/ppermute | solution.py:21
  24.2 2.7 %shard_map.86 = (f32[1024,512]{1,0:T(8,128)S(1)}, f32[1024,512]{1,0:T(8,128)S(1)}, f32[1024,512]{1,0:T(8,128)S(1)}, f32[8,128,128]{2,1,0:T(8,128)S(1)}, f32[12,8...) custom-call(f32[2,4,1024,128]{3,2,1,0:T(8,128)S(1)} %get-tuple-eleme, ...), custom_call_target="tpu_custom_call", output_to_operand_aliasing={{0}: (4, {}), {1}: (5, {}), {2}: (6, {}), {3}: (7, {}), {4}... | custom-call | flops 1000000000 | bytes 3670016 | tf_op jit(solution)/shard_map/pallas_call | solution.py:404
  26.9 0.0 collective-permute-done.6.refs_1_.refs_4_
  26.9 0.2 collective-permute-start.7
  27.1 2.9 %shard_map.87 = (f32[1024,512]{1,0:T(8,128)S(1)}, f32[1024,512]{1,0:T(8,128)S(1)}, f32[1024,512]{1,0:T(8,128)S(1)}, f32[8,128,128]{2,1,0:T(8,128)S(1)}, f32[12,8...) custom-call(f32[2,4,1024,128]{3,2,1,0:T(8,128)S(1)} %get-tuple-eleme, ...), custom_call_target="tpu_custom_call", output_to_operand_aliasing={{0}: (4, {}), {1}: (5, {}), {2}: (6, {}), {3}: (7, {}), {4}... | custom-call | flops 1000000000 | bytes 3670016 | tf_op jit(solution)/shard_map/pallas_call | solution.py:404
  30.1 0.0 collective-permute-done.refs_0_
  30.1 0.0 collective-permute-done.3.refs_1_
  30.1 2.3 %coarse.2 = (f32[1024,512]{1,0:T(8,128)S(1)}, f32[16,1024]{1,0:T(8,128)S(1)}) custom-call(f32[2,4,1024,128]{3,2,1,0:T(8,128)S(1)} %get-tuple-element.44.kq_ref, bf16[2,4,1024,256]{3,2,1,0:T(8,128)(2,1)S(1)} %get-tuple-element.45.right_ref, f32[3,1024,128]{2,1,0:T(8,128)S(1)} %get-tuple-element.70.col_ref, ...), custom_call_target="tpu_custom_call", output_to_operand_aliasing={{0}: (3, {}), {1}: (4, {})} | custom-call | flops 1000000000 | bytes 4194304 | tf_op jit(solution)/shard_map/coarse/pallas_call | solution.py:428
  32.4 0.0 collective-permute-done.7.refs_0_.refs_3_
  32.4 1.4 %coarse.3 = (f32[1024,512]{1,0:T(8,128)S(1)}, f32[16,1024]{1,0:T(8,128)S(1)}) custom-call(f32[2,4,1024,128]{3,2,1,0:T(8,128)S(1)} %get-tuple-element.44.kq_ref, bf16[2,4,1024,256]{3,2,1,0:T(8,128)(2,1)S(1)} %get-tuple-element.45.right_ref, f32[3,1024,128]{2,1,0:T(8,128)S(1)} %get-tuple-element.70.col_ref, ...), custom_call_target="tpu_custom_call", output_to_operand_aliasing={{0}: (3, {}), {1}: (4, {})} | custom-call | flops 1000000000 | bytes 4194304 | tf_op jit(solution)/shard_map/coarse/pallas_call | solution.py:428
  33.7 3.4 %collective-permute-start.8 = (f32[16,1024]{1,0:T(8,128)S(1)}, f32[16,1024]{1,0:T(8,128)S(1)}, u32[]{:S(2)}, u32[]{:S(2)}) collective-permute-start(f32[16,1024]{1,0:T(8,128)S(1)} %get-tuple-element.83), channel_id=1, source_target_pairs={{0,1},{1,0},{2,3},{3,2},{4,5},{5,4},{6,7},{7,6},{8,9},{9,8},{10,11... | collective-permute-start | bytes 196616 | tf_op jit(solution)/shard_map/ppermute | solution.py:21
  37.1 0.9 %collective-permute-done.8 = f32[16,1024]{1,0:T(8,128)S(1)} collective-permute-done((f32[16,1024]{1,0:T(8,128)S(1)}, f32[16,1024]{1,0:T(8,128)S(1)}, u32[]{:S(2)}, u32[]{:S(2)}) %collective-permute-start.8) | collective-permute-done | bytes 65568 | tf_op jit(solution)/shard_map/ppermute | solution.py:21
  38.1 1.3 %collective-permute-start.9 = (f32[16,1024]{1,0:T(8,128)S(1)}, f32[16,1024]{1,0:T(8,128)S(1)}, u32[]{:S(2)}, u32[]{:S(2)}) collective-permute-start(f32[16,1024]{1,0:T(8,128)S(1)} %add.18), channel_id=1, source_target_pairs={{0,2},{1,3},{2,0},{3,1},{4,6},{5,7},{6,4},{7,5},{8,10},{9,11},{10,... | collective-permute-start | bytes 196616 | tf_op jit(solution)/shard_map/ppermute | solution.py:21
  39.4 3.2 %back.1 = (f32[1024,512]{1,0:T(8,128)}, f32[1024,512]{1,0:T(8,128)}, f32[1024,512]{1,0:T(8,128)}) custom-call(f32[2,4,1024,128]{3,2,1,0:T(8,128)S(1)} %get-tuple-element.44.kq_ref, bf16[2,4,1024,256]{3,2,1,0:T(8,128)(2,1)S(1)} %get-tuple-element.45.right_ref, f32[1024,512]{1,0:T(8,128)S(1)} %get-tuple-element.68.old_k, ...), custom_call_target="tpu_custom_call" | custom-call | flops 1000000000 | bytes 8388608 | tf_op jit(solution)/shard_map/back/pallas_call | solution.py:445
  42.6 0.0 collective-permute-done.9
  42.6 0.6 %slice_add_fusion = f32[14,1024]{1,0:T(8,128)} fusion(f32[16,1024]{1,0:T(8,128)S(1)} %collective-permute-done.9, f32[16,1024]{1,0:T(8,128)S(1)} %add.18), kind=kLoop, calls=%fused_computation | loop fusion | flops 14336 | bytes 172032 | tf_op jit(solution)/shard_map/add | solution.py:443
  (4 shorter events, 0.1 us)
Async XLA Ops:
  0.6 11.9 %copy-start = (f32[14,1024]{1,0:T(8,128)S(1)}, f32[14,1024]{1,0:T(8,128)}, u32[]{:S(2)}) copy-start(f32[14,1024]{1,0:T(8,128)} %w_ref.9) | copy-start | bytes 172036
  6.0 5.4 %collective-permute-start.4 = (f32[2,128,128]{2,1,0:T(8,128)S(1)}, f32[2,128,128]{2,1,0:T(8,128)S(1)}, u32[]{:S(2)}, u32[]{:S(2)}) collective-permute-start(f32[2,128,128]{2,1,0:T(8,128)S(1)} %get-tuple-element.78), channel_id=1, source_target_pairs={{0,8},{4,12},{8,0},{12,4},{16,24},{20,28},{24,16},{28,20},{1,9},{5... | collective-permute-start | bytes 393224 | tf_op jit(solution)/shard_map/ppermute | solution.py:21
  8.2 5.7 %collective-permute-start.1 = (f32[2,128,128]{2,1,0:T(8,128)S(1)}, f32[2,128,128]{2,1,0:T(8,128)S(1)}, u32[]{:S(2)}, u32[]{:S(2)}) collective-permute-start(f32[2,128,128]{2,1,0:T(8,128)S(1)} %get-tuple-element.74), channel_id=1, source_target_pairs={{0,4},{4,0},{8,12},{12,8},{16,20},{20,16},{24,28},{28,24},{1,5},{5... | collective-permute-start | bytes 393224 | tf_op jit(solution)/shard_map/ppermute | solution.py:21
  11.4 6.4 %collective-permute-start.5 = (f32[2,128,128]{2,1,0:T(8,128)S(1)}, f32[2,128,128]{2,1,0:T(8,128)S(1)}, u32[]{:S(2)}, u32[]{:S(2)}) collective-permute-start(f32[2,128,128]{2,1,0:T(8,128)S(1)} %add.16), channel_id=1, source_target_pairs={{0,4},{4,0},{8,12},{12,8},{16,20},{20,16},{24,28},{28,24},{1,5},{5... | collective-permute-start | bytes 393224 | tf_op jit(solution)/shard_map/ppermute | solution.py:21
  13.4 16.7 %collective-permute-start = (f32[4,128,128]{2,1,0:T(8,128)S(1)}, f32[4,128,128]{2,1,0:T(8,128)S(1)}, u32[]{:S(2)}, u32[]{:S(2)}) collective-permute-start(f32[4,128,128]{2,1,0:T(8,128)S(1)} %near.1), channel_id=1, source_target_pairs={{0,4},{4,0},{8,12},{12,8},{16,20},{20,16},{24,28},{28,24},{1,5},{5... | collective-permute-start | bytes 786440 | tf_op jit(solution)/shard_map/ppermute | solution.py:21
  13.9 9.1 %collective-permute-start.2 = (f32[2,128,128]{2,1,0:T(8,128)S(1)}, f32[2,128,128]{2,1,0:T(8,128)S(1)}, u32[]{:S(2)}, u32[]{:S(2)}) collective-permute-start(f32[2,128,128]{2,1,0:T(8,128)S(1)} %add.15), channel_id=1, source_target_pairs={{0,8},{4,12},{8,0},{12,4},{16,24},{20,28},{24,16},{28,20},{1,9},{5... | collective-permute-start | bytes 393224 | tf_op jit(solution)/shard_map/ppermute | solution.py:21
  17.9 9.0 %collective-permute-start.6 = (f32[2,128,128]{2,1,0:T(8,128)S(1)}, f32[2,128,128]{2,1,0:T(8,128)S(1)}, u32[]{:S(2)}, u32[]{:S(2)}) collective-permute-start(f32[2,128,128]{2,1,0:T(8,128)S(1)} %add.17), channel_id=1, source_target_pairs={{0,16},{4,20},{8,24},{12,28},{16,0},{20,4},{24,8},{28,12},{1,17},{... | collective-permute-start | bytes 393224 | tf_op jit(solution)/shard_map/ppermute | solution.py:21
  23.0 7.1 %collective-permute-start.3 = (f32[2,128,128]{2,1,0:T(8,128)S(1)}, f32[2,128,128]{2,1,0:T(8,128)S(1)}, u32[]{:S(2)}, u32[]{:S(2)}) collective-permute-start(f32[2,128,128]{2,1,0:T(8,128)S(1)} %collective-permute-done.2.refs_2_), channel_id=1, source_target_pairs={{0,4},{4,0},{8,12},{12,8},{16,20},{20,16},{24,28},{28,24},{1,5},{5... | collective-permute-start | bytes 393224 | tf_op jit(solution)/shard_map/ppermute | solution.py:21
  26.9 5.4 %collective-permute-start.7 = (f32[2,128,128]{2,1,0:T(8,128)S(1)}, f32[2,128,128]{2,1,0:T(8,128)S(1)}, u32[]{:S(2)}, u32[]{:S(2)}) collective-permute-start(f32[2,128,128]{2,1,0:T(8,128)S(1)} %collective-permute-done.6.refs_1_.refs_4_), channel_id=1, source_target_pairs={{0,8},{4,12},{8,0},{12,4},{16,24},{20,28},{24,16},{28,20},{1,9},{5... | collective-permute-start | bytes 393224 | tf_op jit(solution)/shard_map/ppermute | solution.py:21
  33.7 4.3 %collective-permute-start.8 = (f32[16,1024]{1,0:T(8,128)S(1)}, f32[16,1024]{1,0:T(8,128)S(1)}, u32[]{:S(2)}, u32[]{:S(2)}) collective-permute-start(f32[16,1024]{1,0:T(8,128)S(1)} %get-tuple-element.83), channel_id=1, source_target_pairs={{0,1},{1,0},{2,3},{3,2},{4,5},{5,4},{6,7},{7,6},{8,9},{9,8},{10,11... | collective-permute-start | bytes 196616 | tf_op jit(solution)/shard_map/ppermute | solution.py:21
  38.1 4.5 %collective-permute-start.9 = (f32[16,1024]{1,0:T(8,128)S(1)}, f32[16,1024]{1,0:T(8,128)S(1)}, u32[]{:S(2)}, u32[]{:S(2)}) collective-permute-start(f32[16,1024]{1,0:T(8,128)S(1)} %add.18), channel_id=1, source_target_pairs={{0,2},{1,3},{2,0},{3,1},{4,6},{5,7},{6,4},{7,5},{8,10},{9,11},{10,... | collective-permute-start | bytes 196616 | tf_op jit(solution)/shard_map/ppermute | solution.py:21

commit v3 on v2

--- a/solution.py
+++ b/solution.py
@@ -85,7 +85,7 @@
     return dot(grown, tall((right, right)), NN)
 
 
-def state_kernel(first, levels, k_hbm, q_hbm, v_hbm, d_hbm, w_hbm, send_refs, keep_refs, kq_ref, right_ref, turned_ref, w_ref, stage_ref, sum_ref, sems, w_sem):
+def state_kernel(first, levels, k_hbm, q_hbm, v_hbm, d_hbm, w_hbm, send_refs, keep_refs, kq_ref, right_ref, turned_ref, flip_ref, w_ref, stage_ref, sum_ref, sems, w_sem):
     heads, frames = kq_ref.shape[1:3]
     half = heads // 2
 
@@ -119,6 +119,9 @@
                 rights.append(wide(split(stage_ref[i, head, span, :])))
                 turned_ref[i, head, :, span] = turned[i]
                 right_ref[i, head, span, :] = rights[i]
+            for i, x in enumerate((turned[1], stage_ref[1, head, span, :].T)):
+                for c in range(B // C):
+                    flip_ref[i, head, b * (B // C) + c] = wide(split(x[:, c * C : (c + 1) * C]))
             for level in range(1, levels):
                 row = w_ref[first + level : first + level + 1, span]
                 term = product(bit_of(level), row, turned, rights)
@@ -154,12 +157,12 @@
     return x[:, :DK], x[:, DK:]
 
 
-def local_kernel(heads, last, kq_ref, right_ref, turned_ref, w_ref, *refs):
+def local_kernel(heads, last, kq_ref, right_ref, turned_ref, flip_ref, w_ref, *refs):
     start = heads[0] == 0
     if not start:
         refs = refs[7:]
     qg_ref, kg_ref, vg_ref, pr_ref, wc_ref, mix_ref, col_ref = refs[:7]
-    left_ref = refs[-1]
+    left_ref, me_ref, mg_ref = refs[-3:]
     frames = kq_ref.shape[2]
     chunks = frames // C
     heights = chunks.bit_length() - 1
@@ -198,18 +201,37 @@
                 if b << k < chunks - (1 << k):
                     sums[b, k] = sums[2 * b, k - 1] + sums[2 * b + 1, k - 1]
 
-        def scores(c):
-            ks, qs = parts(left_ref, place, 0, spans[c]), parts(left_ref, place, 1, spans[c])
-            vs, ds = right(0, head, spans[c]), right(1, head, spans[c])
-            gt = nt(ks, qs)
-            et = nt(vs, ds)
+        def lefts(c):
+            return parts(left_ref, place, 0, spans[c]), parts(left_ref, place, 1, spans[c])
+
+        for c in range(chunks):
+            ks, qs = lefts(c)
+            gt = nn(ks, parts(flip_ref, 0, head, c))
+            et = nn(right(0, head, spans[c]), parts(flip_ref, 1, head, c))
             add(head, pr_ref, c, gt * et)
             mt = mix_ref[c]
-            return split(mt * et), split(mt * gt)
-
-        def gradients(c, me, mg):
-            ks, qs = parts(left_ref, place, 0, spans[c]), parts(left_ref, place, 1, spans[c])
+            me_ref[spans[c], :] = wide(split(mt * et))
+            mg_ref[spans[c], :] = wide(split(mt * gt))
+        for c in reversed(range(chunks)):
+            ds = right(1, head, spans[c])
+            qt = turned_ref[1, head, :, spans[c]]
+            mixed = None
+            for k in range(heights):
+                if c >> k & 1:
+                    row = w_ref[inner + k : inner + k + 1, spans[c]]
+                    along = nn(split(sums[(c >> k) - 1, k]), parts(flip_ref, 1, head, c))
+                    add(head, wc_ref, pairs.index((c, k)), fold(qt * along))
+                    term = row * along
+                    mixed = term if mixed is None else mixed + term
+                    grad = nn(split(row * qt), ds)
+                    key = ((c >> k) - 1, k)
+                    back[key] = back[key] + grad if key in back else grad
+            if mixed is not None:
+                qg_ref[spans[c], lanes] = mixed.T
+        for c in reversed(range(chunks)):
+            ks, qs = lefts(c)
             vs, ds = right(0, head, spans[c]), right(1, head, spans[c])
+            me, mg = parts(me_ref, spans[c]), parts(mg_ref, spans[c])
             kg, vg, qg = nn(me, qs), nn(mg, ds), tn(me, ks)
             if c < chunks - 1:
                 total = None
@@ -222,29 +244,7 @@
                 vg = vg + nn(ks, bs)
             kg_ref[spans[c], lanes] = kg
             vg_ref[spans[c], lanes] = vg
-            ups = [k for k in range(heights) if c >> k & 1]
-            if ups:
-                qt = turned_ref[1, head, :, spans[c]]
-                mixed = None
-                for k in ups:
-                    row = w_ref[inner + k : inner + k + 1, spans[c]]
-                    along = nt(split(sums[(c >> k) - 1, k]), ds)
-                    add(head, wc_ref, pairs.index((c, k)), fold(qt * along))
-                    term = row * along
-                    mixed = term if mixed is None else mixed + term
-                    grad = nn(split(row * qt), ds)
-                    key = ((c >> k) - 1, k)
-                    back[key] = back[key] + grad if key in back else grad
-                qg = qg + mixed.T
-            qg_ref[spans[c], lanes] = qg
-
-        waiting = None
-        for c in reversed(range(chunks)):
-            now = scores(c)
-            if waiting is not None:
-                gradients(c + 1, *waiting)
-            waiting = now
-        gradients(0, *waiting)
+            qg_ref[spans[c], lanes] = qg_ref[spans[c], lanes] + qg if c else qg
 
     for head in heads:
         inside(head)
@@ -270,29 +270,30 @@
 
 
 def coarse_kernel(first, levels, kq_ref, right_ref, col_ref, old_q, old_w, *refs):
-    arrived, (out_ref, wg_ref, product_ref) = refs[:-3], refs[-3:]
+    arrived, (out_ref, wg_ref) = refs[:-2], refs[-2:]
     heads, frames = kq_ref.shape[1:3]
     arrived = [None] * (2 * levels[-1] + 1 - len(arrived)) + list(arrived)
-    for head in range(heads):
-        lanes = slice(head * DK, (head + 1) * DK)
-        states = []
+    states = {}
+    for head in range(heads):
         for level in levels:
             state = received(level, head, heads // 2, arrived)
-            states.append(split(jnp.where(bit_of(level) == 1, state, 0.0)))
-        for b in range(frames // B):
-            span = slice(b * B, (b + 1) * B)
+            states[head, level] = split(jnp.where(bit_of(level) == 1, state, 0.0))
+    for b in range(frames // B):
+        span = slice(b * B, (b + 1) * B)
+        products = {}
+        for head in range(heads):
+            lanes = slice(head * DK, (head + 1) * DK)
             ds = parts(right_ref, 1, head, span)
             q = kq_ref[1, head, span, :]
             mixed = old_q[span, lanes]
-            for i, level in enumerate(levels):
-                along = nt(ds, states[i])
-                product_ref[i, span, :] = product_ref[i, span, :] + q * along if head else q * along
+            for level in levels:
+                along = nt(ds, states[head, level])
+                share = q * along
+                products[level] = products[level] + share if head else share
                 mixed = mixed + col_ref[level, span, :] * along
             out_ref[span, lanes] = mixed
-    for i, level in enumerate(levels):
-        for c in range(frames // C):
-            span = slice(c * C, (c + 1) * C)
-            row = jnp.sum(product_ref[i, span, :].T, axis=0, keepdims=True)
+        for level in levels:
+            row = jnp.sum(products[level].T, axis=0, keepdims=True)
             wg_ref[first + level : first + level + 1, span] = row
 
 
@@ -360,16 +361,17 @@
     part = jax.ShapeDtypeStruct((half, DK, DK), f32)
     rows = -(-levels // SUB) * SUB
 
-    send, keep, kq, right, turned = pl.pallas_call(
+    send, keep, kq, right, turned, flip = pl.pallas_call(
         functools.partial(state_kernel, fine, device_levels),
         in_specs=[there] * 5,
-        out_specs=[[here] * far] * 2 + [here] * 3,
+        out_specs=[[here] * far] * 2 + [here] * 4,
         out_shape=[
             [part] * far,
             [part] * far,
             pltpu.VMEM((2, heads, frames, DK), f32),
             pltpu.VMEM((2, heads, frames, 2 * DK), bf16),
             pltpu.VMEM((2, heads, DK, frames), f32),
+            pltpu.VMEM((2, heads, chunks, DK, 2 * C), bf16),
         ],
         scratch_shapes=[
             pltpu.VMEM((levels, frames), f32),
@@ -403,14 +405,14 @@
             shapes.append(pltpu.VMEM((rows, frames), f32))
         inner = pl.pallas_call(
             functools.partial(local_kernel, [head], last),
-            in_specs=[here] * (11 if head else 4),
+            in_specs=[here] * (12 if head else 5),
             out_specs=[here] * len(shapes),
             out_shape=shapes,
-            scratch_shapes=[pltpu.VMEM((1, 2, frames, 2 * DK), bf16)],
-            input_output_aliases={4 + j: j for j in range(7)} if head else {},
+            scratch_shapes=[pltpu.VMEM((1, 2, frames, 2 * DK), bf16)] + [pltpu.VMEM((frames, 2 * C), bf16)] * 2,
+            input_output_aliases={5 + j: j for j in range(7)} if head else {},
             compiler_params=params(16),
             cost_estimate=cost(10**9, 7 * block // heads),
-        )(kq, right, turned, level_weights, *(inner or []))
+        )(kq, right, turned, flip, level_weights, *(inner or []))
     q_local, k_local, v_local, _, _, _, columns, weight_grad = inner
 
     states = [partner(near, "tm", 0)]
@@ -430,7 +432,6 @@
             in_specs=[here] * (5 + len(used)),
             out_specs=[here] * 2,
             out_shape=[kept, pltpu.VMEM((rows, frames), f32)],
-            scratch_shapes=[pltpu.VMEM((len(span), frames, DK), f32)],
             input_output_aliases={3: 0, 4: 1},
             compiler_params=params(16),
             cost_estimate=cost(10**9, 2 * block),

time: 44 us -> 41.9 us (0.952)
  Pallas kernels: 24 us -> 21.1 us
  starting transfers between devices: 14.8 us -> 15.6 us
    pallas_call x4, Pallas kernels: 11 us -> 8.03 us  [body(): pl.pallas_call(functools.partial(local_kernel, [head], last), in_specs=[h...]
    ppermute x10, starting transfers between devices: 14.8 us -> 15.6 us  [partner(): lax.ppermute(array, axis, [(i, i ^ 1 << stride) for i in range(lax.axis_s...]
  transfers between devices with their start and end apart: 10 -> 10, of which waited for: 2 -> 2; matrix products, arithmetic and copies ran while one was open for 0% -> 0% of each run, Pallas kernels for 40% -> 35%
where the time goes in v3:
time: 41.9 us; the launch traced here: 41.1 us
  Pallas kernels  21.1 us (50%)
  starting transfers between devices  15.6 us (37%)
  waiting for transfers between devices  2.9 us (7%)
  between operations  0.78 us (2%)
  other arithmetic  0.7 us (2%)
    ppermute x10, starting transfers between devices, partner(): lax.ppermute(array, axis, [(i, i ^ 1 << stride) for i in range(lax.axis_s...  15.6 us
    pallas_call x4, Pallas kernels, body(): pl.pallas_call(functools.partial(local_kernel, [head], last), in_specs=[h...  8.03 us
    pallas_call x1, Pallas kernels, body(): pl.pallas_call(functools.partial(state_kernel, fine, device_levels), in_s...  5.51 us
    pallas_call x2, Pallas kernels, coarse(): pl.pallas_call(functools.partial(coarse_kernel, fine, span), in_specs=[he...  3.58 us
    pallas_call x1, Pallas kernels, body(): pl.pallas_call(functools.partial(back_kernel, device_levels), in_specs=[h...  3.19 us
    ppermute x10, waiting for transfers between devices, partner(): lax.ppermute(array, axis, [(i, i ^ 1 << stride) for i in range(lax.axis_s...  2.9 us
  transfers between devices with their start and end apart: 10, of which 2 were waited for; matrix products, arithmetic and copies ran while one was open for 0% of the time, Pallas kernels for 35%

profile of v3, /device:TPU:1, one launch (start us, length us, event | category | flops | bytes accessed | tf_op | source)
XLA Modules:
  0.0 41.1 jit_solution(10484146698545679094)
XLA Ops:
  0.6 0.0 copy-start
  0.6 5.5 %states.1 = (f32[2,128,128]{2,1,0:T(8,128)S(1)}, f32[2,128,128]{2,1,0:T(8,128)S(1)}, f32[2,128,128]{2,1,0:T(8,128)S(1)}, f32[2,128,128]{2,1,0:T(8,128)S(1)}, f32...) custom-call(f32[1024,512]{1,0:T(8,128)} %k_hbm.1, ...), custom_call_target="tpu_custom_call" | custom-call | flops 1000000000 | bytes 8388608 | tf_op jit(solution)/shard_map/states/pallas_call | solution.py:364
  6.2 2.2 %collective-permute-start.4 = (f32[2,128,128]{2,1,0:T(8,128)S(1)}, f32[2,128,128]{2,1,0:T(8,128)S(1)}, u32[]{:S(2)}, u32[]{:S(2)}) collective-permute-start(f32[2,128,128]{2,1,0:T(8,128)S(1)} %get-tuple-element.80), channel_id=1, source_target_pairs={{0,8},{4,12},{8,0},{12,4},{16,24},{20,28},{24,16},{28,20},{1,9},{5... | collective-permute-start | bytes 393224 | tf_op jit(solution)/shard_map/ppermute | solution.py:21
  8.3 1.2 %collective-permute-start.1 = (f32[2,128,128]{2,1,0:T(8,128)S(1)}, f32[2,128,128]{2,1,0:T(8,128)S(1)}, u32[]{:S(2)}, u32[]{:S(2)}) collective-permute-start(f32[2,128,128]{2,1,0:T(8,128)S(1)} %get-tuple-element.76), channel_id=1, source_target_pairs={{0,4},{4,0},{8,12},{12,8},{16,20},{20,16},{24,28},{28,24},{1,5},{5... | collective-permute-start | bytes 393224 | tf_op jit(solution)/shard_map/ppermute | solution.py:21
  9.6 2.0 %collective-permute-done.4 = f32[2,128,128]{2,1,0:T(8,128)S(1)} collective-permute-done((f32[2,128,128]{2,1,0:T(8,128)S(1)}, f32[2,128,128]{2,1,0:T(8,128)S(1)}, u32[]{:S(2)}, u32[]{:S(2)}) %collective-permute-start.4) | collective-permute-done | bytes 131104 | tf_op jit(solution)/shard_map/ppermute | solution.py:21
  11.6 1.2 %collective-permute-start.5 = (f32[2,128,128]{2,1,0:T(8,128)S(1)}, f32[2,128,128]{2,1,0:T(8,128)S(1)}, u32[]{:S(2)}, u32[]{:S(2)}) collective-permute-start(f32[2,128,128]{2,1,0:T(8,128)S(1)} %add.16), channel_id=1, source_target_pairs={{0,4},{4,0},{8,12},{12,8},{16,20},{20,16},{24,28},{28,24},{1,5},{5... | collective-permute-start | bytes 393224 | tf_op jit(solution)/shard_map/ppermute | solution.py:21
  12.7 0.0 copy-done
  12.7 0.8 %near.1 = f32[4,128,128]{2,1,0:T(8,128)S(1)} custom-call(bf16[2,4,1024,256]{3,2,1,0:T(8,128)(2,1)S(1)} %get-tuple-element.46.right_ref, f32[2,4,128,1024]{3,2,1,0:T(8,128)S(1)} %get-tuple-element.47.turned_ref, f32[14,1024]{1,0:T(8,128)S(1)} %copy-done), custom_call_target="tpu_custom_call" | custom-call | flops 1000000000 | bytes 2097152 | tf_op jit(solution)/shard_map/near/pallas_call | solution.py:388
  13.6 0.4 %collective-permute-start = (f32[4,128,128]{2,1,0:T(8,128)S(1)}, f32[4,128,128]{2,1,0:T(8,128)S(1)}, u32[]{:S(2)}, u32[]{:S(2)}) collective-permute-start(f32[4,128,128]{2,1,0:T(8,128)S(1)} %near.1), channel_id=1, source_target_pairs={{0,4},{4,0},{8,12},{12,8},{16,20},{20,16},{24,28},{28,24},{1,5},{5... | collective-permute-start | bytes 786440 | tf_op jit(solution)/shard_map/ppermute | solution.py:21
  14.0 0.0 collective-permute-done.1
  14.0 1.2 %collective-permute-start.2 = (f32[2,128,128]{2,1,0:T(8,128)S(1)}, f32[2,128,128]{2,1,0:T(8,128)S(1)}, u32[]{:S(2)}, u32[]{:S(2)}) collective-permute-start(f32[2,128,128]{2,1,0:T(8,128)S(1)} %add.15), channel_id=1, source_target_pairs={{0,8},{4,12},{8,0},{12,4},{16,24},{20,28},{24,16},{28,20},{1,9},{5... | collective-permute-start | bytes 393224 | tf_op jit(solution)/shard_map/ppermute | solution.py:21
  15.3 2.0 %shard_map.84 = (f32[1024,512]{1,0:T(8,128)S(1)}, f32[1024,512]{1,0:T(8,128)S(1)}, f32[1024,512]{1,0:T(8,128)S(1)}, f32[8,128,128]{2,1,0:T(8,128)S(1)}, f32[12,8...) custom-call(f32[2,4,1024,128]{3,2,1,0:T(8,128)S(1)} %get-tuple-element.45.kq_ref, ...), custom_call_target="tpu_custom_call" | custom-call | flops 1000000000 | bytes 3670016 | tf_op jit(solution)/shard_map/pallas_call | solution.py:406
  17.2 0.0 collective-permute-done.5
  17.3 2.4 %collective-permute-start.6 = (f32[2,128,128]{2,1,0:T(8,128)S(1)}, f32[2,128,128]{2,1,0:T(8,128)S(1)}, u32[]{:S(2)}, u32[]{:S(2)}) collective-permute-start(f32[2,128,128]{2,1,0:T(8,128)S(1)} %add.17), channel_id=1, source_target_pairs={{0,16},{4,20},{8,24},{12,28},{16,0},{20,4},{24,8},{28,12},{1,17},{... | collective-permute-start | bytes 393224 | tf_op jit(solution)/shard_map/ppermute | solution.py:21
  19.6 1.8 %shard_map.85 = (f32[1024,512]{1,0:T(8,128)S(1)}, f32[1024,512]{1,0:T(8,128)S(1)}, f32[1024,512]{1,0:T(8,128)S(1)}, f32[8,128,128]{2,1,0:T(8,128)S(1)}, f32[12,8...) custom-call(f32[2,4,1024,128]{3,2,1,0:T(8,128)S(1)} %get-tuple-eleme, ...), custom_call_target="tpu_custom_call", output_to_operand_aliasing={{0}: (5, {}), {1}: (6, {}), {2}: (7, {}), {3}: (8, {}), {4}... | custom-call | flops 1000000000 | bytes 3670016 | tf_op jit(solution)/shard_map/pallas_call | solution.py:406
  21.5 0.0 collective-permute-done.2.refs_2_
  21.5 1.3 %collective-permute-start.3 = (f32[2,128,128]{2,1,0:T(8,128)S(1)}, f32[2,128,128]{2,1,0:T(8,128)S(1)}, u32[]{:S(2)}, u32[]{:S(2)}) collective-permute-start(f32[2,128,128]{2,1,0:T(8,128)S(1)} %collective-permute-done.2.refs_2_), channel_id=1, source_target_pairs={{0,4},{4,0},{8,12},{12,8},{16,20},{20,16},{24,28},{28,24},{1,5},{5... | collective-permute-start | bytes 393224 | tf_op jit(solution)/shard_map/ppermute | solution.py:21
  22.7 1.8 %shard_map.86 = (f32[1024,512]{1,0:T(8,128)S(1)}, f32[1024,512]{1,0:T(8,128)S(1)}, f32[1024,512]{1,0:T(8,128)S(1)}, f32[8,128,128]{2,1,0:T(8,128)S(1)}, f32[12,8...) custom-call(f32[2,4,1024,128]{3,2,1,0:T(8,128)S(1)} %get-tuple-eleme, ...), custom_call_target="tpu_custom_call", output_to_operand_aliasing={{0}: (5, {}), {1}: (6, {}), {2}: (7, {}), {3}: (8, {}), {4}... | custom-call | flops 1000000000 | bytes 3670016 | tf_op jit(solution)/shard_map/pallas_call | solution.py:406
  24.6 0.0 collective-permute-done.6.refs_1_.refs_4_
  24.6 0.2 collective-permute-start.7
  24.8 2.4 %shard_map.87 = (f32[1024,512]{1,0:T(8,128)S(1)}, f32[1024,512]{1,0:T(8,128)S(1)}, f32[1024,512]{1,0:T(8,128)S(1)}, f32[8,128,128]{2,1,0:T(8,128)S(1)}, f32[12,8...) custom-call(f32[2,4,1024,128]{3,2,1,0:T(8,128)S(1)} %get-tuple-eleme, ...), custom_call_target="tpu_custom_call", output_to_operand_aliasing={{0}: (5, {}), {1}: (6, {}), {2}: (7, {}), {3}: (8, {}), {4}... | custom-call | flops 1000000000 | bytes 3670016 | tf_op jit(solution)/shard_map/pallas_call | solution.py:406
  27.3 0.0 collective-permute-done.refs_0_
  27.3 0.0 collective-permute-done.3.refs_1_
  27.3 2.3 %coarse.2 = (f32[1024,512]{1,0:T(8,128)S(1)}, f32[16,1024]{1,0:T(8,128)S(1)}) custom-call(f32[2,4,1024,128]{3,2,1,0:T(8,128)S(1)} %get-tuple-element.45.kq_ref, bf16[2,4,1024,256]{3,2,1,0:T(8,128)(2,1)S(1)} %get-tuple-element.46.right_ref, f32[3,1024,128]{2,1,0:T(8,128)S(1)} %get-tuple-element.72.col_ref, ...), custom_call_target="tpu_custom_call", output_to_operand_aliasing={{0}: (3, {}), {1}: (4, {})} | custom-call | flops 1000000000 | bytes 4194304 | tf_op jit(solution)/shard_map/coarse/pallas_call | solution.py:430
  29.6 0.0 collective-permute-done.7.refs_0_.refs_3_
  29.6 1.2 %coarse.3 = (f32[1024,512]{1,0:T(8,128)S(1)}, f32[16,1024]{1,0:T(8,128)S(1)}) custom-call(f32[2,4,1024,128]{3,2,1,0:T(8,128)S(1)} %get-tuple-element.45.kq_ref, bf16[2,4,1024,256]{3,2,1,0:T(8,128)(2,1)S(1)} %get-tuple-element.46.right_ref, f32[3,1024,128]{2,1,0:T(8,128)S(1)} %get-tuple-element.72.col_ref, ...), custom_call_target="tpu_custom_call", output_to_operand_aliasing={{0}: (3, {}), {1}: (4, {})} | custom-call | flops 1000000000 | bytes 4194304 | tf_op jit(solution)/shard_map/coarse/pallas_call | solution.py:430
  30.9 4.2 %collective-permute-start.8 = (f32[16,1024]{1,0:T(8,128)S(1)}, f32[16,1024]{1,0:T(8,128)S(1)}, u32[]{:S(2)}, u32[]{:S(2)}) collective-permute-start(f32[16,1024]{1,0:T(8,128)S(1)} %get-tuple-element.85), channel_id=1, source_target_pairs={{0,1},{1,0},{2,3},{3,2},{4,5},{5,4},{6,7},{7,6},{8,9},{9,8},{10,11... | collective-permute-start | bytes 196616 | tf_op jit(solution)/shard_map/ppermute | solution.py:21
  35.1 0.9 %collective-permute-done.8 = f32[16,1024]{1,0:T(8,128)S(1)} collective-permute-done((f32[16,1024]{1,0:T(8,128)S(1)}, f32[16,1024]{1,0:T(8,128)S(1)}, u32[]{:S(2)}, u32[]{:S(2)}) %collective-permute-start.8) | collective-permute-done | bytes 65568 | tf_op jit(solution)/shard_map/ppermute | solution.py:21
  36.0 1.3 %collective-permute-start.9 = (f32[16,1024]{1,0:T(8,128)S(1)}, f32[16,1024]{1,0:T(8,128)S(1)}, u32[]{:S(2)}, u32[]{:S(2)}) collective-permute-start(f32[16,1024]{1,0:T(8,128)S(1)} %add.18), channel_id=1, source_target_pairs={{0,2},{1,3},{2,0},{3,1},{4,6},{5,7},{6,4},{7,5},{8,10},{9,11},{10,... | collective-permute-start | bytes 196616 | tf_op jit(solution)/shard_map/ppermute | solution.py:21
  37.3 3.2 %back.1 = (f32[1024,512]{1,0:T(8,128)}, f32[1024,512]{1,0:T(8,128)}, f32[1024,512]{1,0:T(8,128)}) custom-call(f32[2,4,1024,128]{3,2,1,0:T(8,128)S(1)} %get-tuple-element.45.kq_ref, bf16[2,4,1024,256]{3,2,1,0:T(8,128)(2,1)S(1)} %get-tuple-element.46.right_ref, f32[1024,512]{1,0:T(8,128)S(1)} %get-tuple-element.70.old_k, ...), custom_call_target="tpu_custom_call" | custom-call | flops 1000000000 | bytes 8388608 | tf_op jit(solution)/shard_map/back/pallas_call | solution.py:446
  40.5 0.0 collective-permute-done.9
  40.5 0.6 %slice_add_fusion = f32[14,1024]{1,0:T(8,128)} fusion(f32[16,1024]{1,0:T(8,128)S(1)} %collective-permute-done.9, f32[16,1024]{1,0:T(8,128)S(1)} %add.18), kind=kLoop, calls=%fused_computation | loop fusion | flops 14336 | bytes 172032 | tf_op jit(solution)/shard_map/add | solution.py:444
  (4 shorter events, 0.1 us)
Async XLA Ops:
  0.6 12.1 %copy-start = (f32[14,1024]{1,0:T(8,128)S(1)}, f32[14,1024]{1,0:T(8,128)}, u32[]{:S(2)}) copy-start(f32[14,1024]{1,0:T(8,128)} %w_ref.9) | copy-start | bytes 172036
  6.2 5.4 %collective-permute-start.4 = (f32[2,128,128]{2,1,0:T(8,128)S(1)}, f32[2,128,128]{2,1,0:T(8,128)S(1)}, u32[]{:S(2)}, u32[]{:S(2)}) collective-permute-start(f32[2,128,128]{2,1,0:T(8,128)S(1)} %get-tuple-element.80), channel_id=1, source_target_pairs={{0,8},{4,12},{8,0},{12,4},{16,24},{20,28},{24,16},{28,20},{1,9},{5... | collective-permute-start | bytes 393224 | tf_op jit(solution)/shard_map/ppermute | solution.py:21
  8.3 5.7 %collective-permute-start.1 = (f32[2,128,128]{2,1,0:T(8,128)S(1)}, f32[2,128,128]{2,1,0:T(8,128)S(1)}, u32[]{:S(2)}, u32[]{:S(2)}) collective-permute-start(f32[2,128,128]{2,1,0:T(8,128)S(1)} %get-tuple-element.76), channel_id=1, source_target_pairs={{0,4},{4,0},{8,12},{12,8},{16,20},{20,16},{24,28},{28,24},{1,5},{5... | collective-permute-start | bytes 393224 | tf_op jit(solution)/shard_map/ppermute | solution.py:21
  11.6 5.7 %collective-permute-start.5 = (f32[2,128,128]{2,1,0:T(8,128)S(1)}, f32[2,128,128]{2,1,0:T(8,128)S(1)}, u32[]{:S(2)}, u32[]{:S(2)}) collective-permute-start(f32[2,128,128]{2,1,0:T(8,128)S(1)} %add.16), channel_id=1, source_target_pairs={{0,4},{4,0},{8,12},{12,8},{16,20},{20,16},{24,28},{28,24},{1,5},{5... | collective-permute-start | bytes 393224 | tf_op jit(solution)/shard_map/ppermute | solution.py:21
  13.6 13.7 %collective-permute-start = (f32[4,128,128]{2,1,0:T(8,128)S(1)}, f32[4,128,128]{2,1,0:T(8,128)S(1)}, u32[]{:S(2)}, u32[]{:S(2)}) collective-permute-start(f32[4,128,128]{2,1,0:T(8,128)S(1)} %near.1), channel_id=1, source_target_pairs={{0,4},{4,0},{8,12},{12,8},{16,20},{20,16},{24,28},{28,24},{1,5},{5... | collective-permute-start | bytes 786440 | tf_op jit(solution)/shard_map/ppermute | solution.py:21
  14.0 7.4 %collective-permute-start.2 = (f32[2,128,128]{2,1,0:T(8,128)S(1)}, f32[2,128,128]{2,1,0:T(8,128)S(1)}, u32[]{:S(2)}, u32[]{:S(2)}) collective-permute-start(f32[2,128,128]{2,1,0:T(8,128)S(1)} %add.15), channel_id=1, source_target_pairs={{0,8},{4,12},{8,0},{12,4},{16,24},{20,28},{24,16},{28,20},{1,9},{5... | collective-permute-start | bytes 393224 | tf_op jit(solution)/shard_map/ppermute | solution.py:21
  17.3 7.3 %collective-permute-start.6 = (f32[2,128,128]{2,1,0:T(8,128)S(1)}, f32[2,128,128]{2,1,0:T(8,128)S(1)}, u32[]{:S(2)}, u32[]{:S(2)}) collective-permute-start(f32[2,128,128]{2,1,0:T(8,128)S(1)} %add.17), channel_id=1, source_target_pairs={{0,16},{4,20},{8,24},{12,28},{16,0},{20,4},{24,8},{28,12},{1,17},{... | collective-permute-start | bytes 393224 | tf_op jit(solution)/shard_map/ppermute | solution.py:21
  21.5 5.8 %collective-permute-start.3 = (f32[2,128,128]{2,1,0:T(8,128)S(1)}, f32[2,128,128]{2,1,0:T(8,128)S(1)}, u32[]{:S(2)}, u32[]{:S(2)}) collective-permute-start(f32[2,128,128]{2,1,0:T(8,128)S(1)} %collective-permute-done.2.refs_2_), channel_id=1, source_target_pairs={{0,4},{4,0},{8,12},{12,8},{16,20},{20,16},{24,28},{28,24},{1,5},{5... | collective-permute-start | bytes 393224 | tf_op jit(solution)/shard_map/ppermute | solution.py:21
  24.6 5.0 %collective-permute-start.7 = (f32[2,128,128]{2,1,0:T(8,128)S(1)}, f32[2,128,128]{2,1,0:T(8,128)S(1)}, u32[]{:S(2)}, u32[]{:S(2)}) collective-permute-start(f32[2,128,128]{2,1,0:T(8,128)S(1)} %collective-permute-done.6.refs_1_.refs_4_), channel_id=1, source_target_pairs={{0,8},{4,12},{8,0},{12,4},{16,24},{20,28},{24,16},{28,20},{1,9},{5... | collective-permute-start | bytes 393224 | tf_op jit(solution)/shard_map/ppermute | solution.py:21
  30.9 5.1 %collective-permute-start.8 = (f32[16,1024]{1,0:T(8,128)S(1)}, f32[16,1024]{1,0:T(8,128)S(1)}, u32[]{:S(2)}, u32[]{:S(2)}) collective-permute-start(f32[16,1024]{1,0:T(8,128)S(1)} %get-tuple-element.85), channel_id=1, source_target_pairs={{0,1},{1,0},{2,3},{3,2},{4,5},{5,4},{6,7},{7,6},{8,9},{9,8},{10,11... | collective-permute-start | bytes 196616 | tf_op jit(solution)/shard_map/ppermute | solution.py:21
  36.0 4.5 %collective-permute-start.9 = (f32[16,1024]{1,0:T(8,128)S(1)}, f32[16,1024]{1,0:T(8,128)S(1)}, u32[]{:S(2)}, u32[]{:S(2)}) collective-permute-start(f32[16,1024]{1,0:T(8,128)S(1)} %add.18), channel_id=1, source_target_pairs={{0,2},{1,3},{2,0},{3,1},{4,6},{5,7},{6,4},{7,5},{8,10},{9,11},{10,... | collective-permute-start | bytes 196616 | tf_op jit(solution)/shard_map/ppermute | solution.py:21

commit v4 on v3

--- a/solution.py
+++ b/solution.py
@@ -85,7 +85,7 @@
     return dot(grown, tall((right, right)), NN)
 
 
-def state_kernel(first, levels, k_hbm, q_hbm, v_hbm, d_hbm, w_hbm, send_refs, keep_refs, kq_ref, right_ref, turned_ref, flip_ref, w_ref, stage_ref, sum_ref, sems, w_sem):
+def state_kernel(first, levels, k_hbm, q_hbm, v_hbm, d_hbm, w_hbm, send_refs, keep_refs, kq_ref, right_ref, turned_ref, w_ref, stage_ref, sum_ref, sems, w_sem):
     heads, frames = kq_ref.shape[1:3]
     half = heads // 2
 
@@ -119,9 +119,6 @@
                 rights.append(wide(split(stage_ref[i, head, span, :])))
                 turned_ref[i, head, :, span] = turned[i]
                 right_ref[i, head, span, :] = rights[i]
-            for i, x in enumerate((turned[1], stage_ref[1, head, span, :].T)):
-                for c in range(B // C):
-                    flip_ref[i, head, b * (B // C) + c] = wide(split(x[:, c * C : (c + 1) * C]))
             for level in range(1, levels):
                 row = w_ref[first + level : first + level + 1, span]
                 term = product(bit_of(level), row, turned, rights)
@@ -157,12 +154,12 @@
     return x[:, :DK], x[:, DK:]
 
 
-def local_kernel(heads, last, kq_ref, right_ref, turned_ref, flip_ref, w_ref, *refs):
+def local_kernel(heads, last, kq_ref, right_ref, turned_ref, w_ref, *refs):
     start = heads[0] == 0
     if not start:
         refs = refs[7:]
     qg_ref, kg_ref, vg_ref, pr_ref, wc_ref, mix_ref, col_ref = refs[:7]
-    left_ref, me_ref, mg_ref = refs[-3:]
+    left_ref, me_ref, mg_ref, flip_ref = refs[-4:]
     frames = kq_ref.shape[2]
     chunks = frames // C
     heights = chunks.bit_length() - 1
@@ -194,6 +191,8 @@
         for c in range(chunks):
             for i in range(2):
                 left_ref[place, i, spans[c], :] = wide(split(kq_ref[i, head, spans[c], :]))
+            flip_ref[0, c] = wide(split(turned_ref[1, head, :, spans[c]]))
+            flip_ref[1, c] = wide([x.T for x in right(1, head, spans[c])])
         for c in range(chunks - 1):
             sums[c, 0] = tn(parts(left_ref, place, 0, spans[c]), right(0, head, spans[c]))
         for k in range(1, heights):
@@ -206,8 +205,8 @@
 
         for c in range(chunks):
             ks, qs = lefts(c)
-            gt = nn(ks, parts(flip_ref, 0, head, c))
-            et = nn(right(0, head, spans[c]), parts(flip_ref, 1, head, c))
+            gt = nn(ks, parts(flip_ref, 0, c))
+            et = nn(right(0, head, spans[c]), parts(flip_ref, 1, c))
             add(head, pr_ref, c, gt * et)
             mt = mix_ref[c]
             me_ref[spans[c], :] = wide(split(mt * et))
@@ -219,7 +218,7 @@
             for k in range(heights):
                 if c >> k & 1:
                     row = w_ref[inner + k : inner + k + 1, spans[c]]
-                    along = nn(split(sums[(c >> k) - 1, k]), parts(flip_ref, 1, head, c))
+                    along = nn(split(sums[(c >> k) - 1, k]), parts(flip_ref, 1, c))
                     add(head, wc_ref, pairs.index((c, k)), fold(qt * along))
                     term = row * along
                     mixed = term if mixed is None else mixed + term
@@ -361,17 +360,16 @@
     part = jax.ShapeDtypeStruct((half, DK, DK), f32)
     rows = -(-levels // SUB) * SUB
 
-    send, keep, kq, right, turned, flip = pl.pallas_call(
+    send, keep, kq, right, turned = pl.pallas_call(
         functools.partial(state_kernel, fine, device_levels),
         in_specs=[there] * 5,
-        out_specs=[[here] * far] * 2 + [here] * 4,
+        out_specs=[[here] * far] * 2 + [here] * 3,
         out_shape=[
             [part] * far,
             [part] * far,
             pltpu.VMEM((2, heads, frames, DK), f32),
             pltpu.VMEM((2, heads, frames, 2 * DK), bf16),
             pltpu.VMEM((2, heads, DK, frames), f32),
-            pltpu.VMEM((2, heads, chunks, DK, 2 * C), bf16),
         ],
         scratch_shapes=[
             pltpu.VMEM((levels, frames), f32),
@@ -405,14 +403,16 @@
             shapes.append(pltpu.VMEM((rows, frames), f32))
         inner = pl.pallas_call(
             functools.partial(local_kernel, [head], last),
-            in_specs=[here] * (12 if head else 5),
+            in_specs=[here] * (11 if head else 4),
             out_specs=[here] * len(shapes),
             out_shape=shapes,
-            scratch_shapes=[pltpu.VMEM((1, 2, frames, 2 * DK), bf16)] + [pltpu.VMEM((frames, 2 * C), bf16)] * 2,
-            input_output_aliases={5 + j: j for j in range(7)} if head else {},
+            scratch_shapes=[pltpu.VMEM((1, 2, frames, 2 * DK), bf16)]
+            + [pltpu.VMEM((frames, 2 * C), bf16)] * 2
+            + [pltpu.VMEM((2, chunks, DK, 2 * C), bf16)],
+            input_output_aliases={4 + j: j for j in range(7)} if head else {},
             compiler_params=params(16),
             cost_estimate=cost(10**9, 7 * block // heads),
-        )(kq, right, turned, flip, level_weights, *(inner or []))
+        )(kq, right, turned, level_weights, *(inner or []))
     q_local, k_local, v_local, _, _, _, columns, weight_grad = inner
 
     states = [partner(near, "tm", 0)]

time: 41.9 us -> 41.7 us (level)
  no operation moved by 1% of the time
where the time goes in v4:
time: 41.7 us; the launch traced here: 41 us
  Pallas kernels  21 us (50%)
  starting transfers between devices  15.6 us (37%)
  waiting for transfers between devices  2.92 us (7%)
  between operations  0.78 us (2%)
  other arithmetic  0.7 us (2%)
    ppermute x10, starting transfers between devices, partner(): lax.ppermute(array, axis, [(i, i ^ 1 << stride) for i in range(lax.axis_s...  15.6 us
    pallas_call x4, Pallas kernels, body(): pl.pallas_call(functools.partial(local_kernel, [head], last), in_specs=[h...  7.87 us
    pallas_call x1, Pallas kernels, body(): pl.pallas_call(functools.partial(state_kernel, fine, device_levels), in_s...  5.33 us
    pallas_call x2, Pallas kernels, coarse(): pl.pallas_call(functools.partial(coarse_kernel, fine, span), in_specs=[he...  3.77 us
    pallas_call x1, Pallas kernels, body(): pl.pallas_call(functools.partial(back_kernel, device_levels), in_specs=[h...  3.18 us
    ppermute x10, waiting for transfers between devices, partner(): lax.ppermute(array, axis, [(i, i ^ 1 << stride) for i in range(lax.axis_s...  2.92 us
    pallas_call x1, Pallas kernels, body(): pl.pallas_call(functools.partial(near_kernel, fine), in_specs=[here] * 3,...  0.84 us
  transfers between devices with their start and end apart: 10, of which 2 were waited for; matrix products, arithmetic and copies ran while one was open for 0% of the time, Pallas kernels for 35%

profile of v4, /device:TPU:1, one launch (start us, length us, event | category | flops | bytes accessed | tf_op | source)
XLA Modules:
  0.0 41.0 jit_solution(1317758637257901126)
XLA Ops:
  0.6 0.0 copy-start
  0.6 5.3 %states.1 = (f32[2,128,128]{2,1,0:T(8,128)S(1)}, f32[2,128,128]{2,1,0:T(8,128)S(1)}, f32[2,128,128]{2,1,0:T(8,128)S(1)}, f32[2,128,128]{2,1,0:T(8,128)S(1)}, f32...) custom-call(f32[1024,512]{1,0:T(8,128)} %k_hbm.1, ...), custom_call_target="tpu_custom_call" | custom-call | flops 1000000000 | bytes 8388608 | tf_op jit(solution)/shard_map/states/pallas_call | solution.py:363
  6.0 2.2 %collective-permute-start.4 = (f32[2,128,128]{2,1,0:T(8,128)S(1)}, f32[2,128,128]{2,1,0:T(8,128)S(1)}, u32[]{:S(2)}, u32[]{:S(2)}) collective-permute-start(f32[2,128,128]{2,1,0:T(8,128)S(1)} %get-tuple-element.78), channel_id=1, source_target_pairs={{0,8},{4,12},{8,0},{12,4},{16,24},{20,28},{24,16},{28,20},{1,9},{5... | collective-permute-start | bytes 393224 | tf_op jit(solution)/shard_map/ppermute | solution.py:21
  8.2 1.2 %collective-permute-start.1 = (f32[2,128,128]{2,1,0:T(8,128)S(1)}, f32[2,128,128]{2,1,0:T(8,128)S(1)}, u32[]{:S(2)}, u32[]{:S(2)}) collective-permute-start(f32[2,128,128]{2,1,0:T(8,128)S(1)} %get-tuple-element.74), channel_id=1, source_target_pairs={{0,4},{4,0},{8,12},{12,8},{16,20},{20,16},{24,28},{28,24},{1,5},{5... | collective-permute-start | bytes 393224 | tf_op jit(solution)/shard_map/ppermute | solution.py:21
  9.4 2.0 %collective-permute-done.4 = f32[2,128,128]{2,1,0:T(8,128)S(1)} collective-permute-done((f32[2,128,128]{2,1,0:T(8,128)S(1)}, f32[2,128,128]{2,1,0:T(8,128)S(1)}, u32[]{:S(2)}, u32[]{:S(2)}) %collective-permute-start.4) | collective-permute-done | bytes 131104 | tf_op jit(solution)/shard_map/ppermute | solution.py:21
  11.4 1.1 %collective-permute-start.5 = (f32[2,128,128]{2,1,0:T(8,128)S(1)}, f32[2,128,128]{2,1,0:T(8,128)S(1)}, u32[]{:S(2)}, u32[]{:S(2)}) collective-permute-start(f32[2,128,128]{2,1,0:T(8,128)S(1)} %add.16), channel_id=1, source_target_pairs={{0,4},{4,0},{8,12},{12,8},{16,20},{20,16},{24,28},{28,24},{1,5},{5... | collective-permute-start | bytes 393224 | tf_op jit(solution)/shard_map/ppermute | solution.py:21
  12.5 0.0 copy-done
  12.5 0.8 %near.1 = f32[4,128,128]{2,1,0:T(8,128)S(1)} custom-call(bf16[2,4,1024,256]{3,2,1,0:T(8,128)(2,1)S(1)} %get-tuple-element.45.right_ref, f32[2,4,128,1024]{3,2,1,0:T(8,128)S(1)} %get-tuple-element.46.turned_ref, f32[14,1024]{1,0:T(8,128)S(1)} %copy-done), custom_call_target="tpu_custom_call" | custom-call | flops 1000000000 | bytes 2097152 | tf_op jit(solution)/shard_map/near/pallas_call | solution.py:386
  13.4 0.5 %collective-permute-start = (f32[4,128,128]{2,1,0:T(8,128)S(1)}, f32[4,128,128]{2,1,0:T(8,128)S(1)}, u32[]{:S(2)}, u32[]{:S(2)}) collective-permute-start(f32[4,128,128]{2,1,0:T(8,128)S(1)} %near.1), channel_id=1, source_target_pairs={{0,4},{4,0},{8,12},{12,8},{16,20},{20,16},{24,28},{28,24},{1,5},{5... | collective-permute-start | bytes 786440 | tf_op jit(solution)/shard_map/ppermute | solution.py:21
  13.8 0.0 collective-permute-done.1
  13.8 1.2 %collective-permute-start.2 = (f32[2,128,128]{2,1,0:T(8,128)S(1)}, f32[2,128,128]{2,1,0:T(8,128)S(1)}, u32[]{:S(2)}, u32[]{:S(2)}) collective-permute-start(f32[2,128,128]{2,1,0:T(8,128)S(1)} %add.15), channel_id=1, source_target_pairs={{0,8},{4,12},{8,0},{12,4},{16,24},{20,28},{24,16},{28,20},{1,9},{5... | collective-permute-start | bytes 393224 | tf_op jit(solution)/shard_map/ppermute | solution.py:21
  15.1 2.0 %shard_map.84 = (f32[1024,512]{1,0:T(8,128)S(1)}, f32[1024,512]{1,0:T(8,128)S(1)}, f32[1024,512]{1,0:T(8,128)S(1)}, f32[8,128,128]{2,1,0:T(8,128)S(1)}, f32[12,8...) custom-call(f32[2,4,1024,128]{3,2,1,0:T(8,128)S(1)} %get-tuple-element.44.kq_ref, ...), custom_call_target="tpu_custom_call" | custom-call | flops 1000000000 | bytes 3670016 | tf_op jit(solution)/shard_map/pallas_call | solution.py:404
  17.1 0.0 collective-permute-done.5
  17.1 2.4 %collective-permute-start.6 = (f32[2,128,128]{2,1,0:T(8,128)S(1)}, f32[2,128,128]{2,1,0:T(8,128)S(1)}, u32[]{:S(2)}, u32[]{:S(2)}) collective-permute-start(f32[2,128,128]{2,1,0:T(8,128)S(1)} %add.17), channel_id=1, source_target_pairs={{0,16},{4,20},{8,24},{12,28},{16,0},{20,4},{24,8},{28,12},{1,17},{... | collective-permute-start | bytes 393224 | tf_op jit(solution)/shard_map/ppermute | solution.py:21
  19.5 1.8 %shard_map.85 = (f32[1024,512]{1,0:T(8,128)S(1)}, f32[1024,512]{1,0:T(8,128)S(1)}, f32[1024,512]{1,0:T(8,128)S(1)}, f32[8,128,128]{2,1,0:T(8,128)S(1)}, f32[12,8...) custom-call(f32[2,4,1024,128]{3,2,1,0:T(8,128)S(1)} %get-tuple-eleme, ...), custom_call_target="tpu_custom_call", output_to_operand_aliasing={{0}: (4, {}), {1}: (5, {}), {2}: (6, {}), {3}: (7, {}), {4}... | custom-call | flops 1000000000 | bytes 3670016 | tf_op jit(solution)/shard_map/pallas_call | solution.py:404
  21.3 0.0 collective-permute-done.2.refs_2_
  21.3 1.3 %collective-permute-start.3 = (f32[2,128,128]{2,1,0:T(8,128)S(1)}, f32[2,128,128]{2,1,0:T(8,128)S(1)}, u32[]{:S(2)}, u32[]{:S(2)}) collective-permute-start(f32[2,128,128]{2,1,0:T(8,128)S(1)} %collective-permute-done.2.refs_2_), channel_id=1, source_target_pairs={{0,4},{4,0},{8,12},{12,8},{16,20},{20,16},{24,28},{28,24},{1,5},{5... | collective-permute-start | bytes 393224 | tf_op jit(solution)/shard_map/ppermute | solution.py:21
  22.6 1.8 %shard_map.86 = (f32[1024,512]{1,0:T(8,128)S(1)}, f32[1024,512]{1,0:T(8,128)S(1)}, f32[1024,512]{1,0:T(8,128)S(1)}, f32[8,128,128]{2,1,0:T(8,128)S(1)}, f32[12,8...) custom-call(f32[2,4,1024,128]{3,2,1,0:T(8,128)S(1)} %get-tuple-eleme, ...), custom_call_target="tpu_custom_call", output_to_operand_aliasing={{0}: (4, {}), {1}: (5, {}), {2}: (6, {}), {3}: (7, {}), {4}... | custom-call | flops 1000000000 | bytes 3670016 | tf_op jit(solution)/shard_map/pallas_call | solution.py:404
  24.4 0.0 collective-permute-done.6.refs_1_.refs_4_
  24.4 0.2 collective-permute-start.7
  24.7 2.3 %shard_map.87 = (f32[1024,512]{1,0:T(8,128)S(1)}, f32[1024,512]{1,0:T(8,128)S(1)}, f32[1024,512]{1,0:T(8,128)S(1)}, f32[8,128,128]{2,1,0:T(8,128)S(1)}, f32[12,8...) custom-call(f32[2,4,1024,128]{3,2,1,0:T(8,128)S(1)} %get-tuple-eleme, ...), custom_call_target="tpu_custom_call", output_to_operand_aliasing={{0}: (4, {}), {1}: (5, {}), {2}: (6, {}), {3}: (7, {}), {4}... | custom-call | flops 1000000000 | bytes 3670016 | tf_op jit(solution)/shard_map/pallas_call | solution.py:404
  26.9 0.0 collective-permute-done.refs_0_
  26.9 0.0 collective-permute-done.3.refs_1_
  26.9 2.5 %coarse.2 = (f32[1024,512]{1,0:T(8,128)S(1)}, f32[16,1024]{1,0:T(8,128)S(1)}) custom-call(f32[2,4,1024,128]{3,2,1,0:T(8,128)S(1)} %get-tuple-element.44.kq_ref, bf16[2,4,1024,256]{3,2,1,0:T(8,128)(2,1)S(1)} %get-tuple-element.45.right_ref, f32[3,1024,128]{2,1,0:T(8,128)S(1)} %get-tuple-element.70.col_ref, ...), custom_call_target="tpu_custom_call", output_to_operand_aliasing={{0}: (3, {}), {1}: (4, {})} | custom-call | flops 1000000000 | bytes 4194304 | tf_op jit(solution)/shard_map/coarse/pallas_call | solution.py:430
  29.5 0.0 collective-permute-done.7.refs_0_.refs_3_
  29.5 1.2 %coarse.3 = (f32[1024,512]{1,0:T(8,128)S(1)}, f32[16,1024]{1,0:T(8,128)S(1)}) custom-call(f32[2,4,1024,128]{3,2,1,0:T(8,128)S(1)} %get-tuple-element.44.kq_ref, bf16[2,4,1024,256]{3,2,1,0:T(8,128)(2,1)S(1)} %get-tuple-element.45.right_ref, f32[3,1024,128]{2,1,0:T(8,128)S(1)} %get-tuple-element.70.col_ref, ...), custom_call_target="tpu_custom_call", output_to_operand_aliasing={{0}: (3, {}), {1}: (4, {})} | custom-call | flops 1000000000 | bytes 4194304 | tf_op jit(solution)/shard_map/coarse/pallas_call | solution.py:430
  30.7 4.2 %collective-permute-start.8 = (f32[16,1024]{1,0:T(8,128)S(1)}, f32[16,1024]{1,0:T(8,128)S(1)}, u32[]{:S(2)}, u32[]{:S(2)}) collective-permute-start(f32[16,1024]{1,0:T(8,128)S(1)} %get-tuple-element.83), channel_id=1, source_target_pairs={{0,1},{1,0},{2,3},{3,2},{4,5},{5,4},{6,7},{7,6},{8,9},{9,8},{10,11... | collective-permute-start | bytes 196616 | tf_op jit(solution)/shard_map/ppermute | solution.py:21
  34.9 0.9 %collective-permute-done.8 = f32[16,1024]{1,0:T(8,128)S(1)} collective-permute-done((f32[16,1024]{1,0:T(8,128)S(1)}, f32[16,1024]{1,0:T(8,128)S(1)}, u32[]{:S(2)}, u32[]{:S(2)}) %collective-permute-start.8) | collective-permute-done | bytes 65568 | tf_op jit(solution)/shard_map/ppermute | solution.py:21
  35.8 1.3 %collective-permute-start.9 = (f32[16,1024]{1,0:T(8,128)S(1)}, f32[16,1024]{1,0:T(8,128)S(1)}, u32[]{:S(2)}, u32[]{:S(2)}) collective-permute-start(f32[16,1024]{1,0:T(8,128)S(1)} %add.18), channel_id=1, source_target_pairs={{0,2},{1,3},{2,0},{3,1},{4,6},{5,7},{6,4},{7,5},{8,10},{9,11},{10,... | collective-permute-start | bytes 196616 | tf_op jit(solution)/shard_map/ppermute | solution.py:21
  37.1 3.2 %back.1 = (f32[1024,512]{1,0:T(8,128)}, f32[1024,512]{1,0:T(8,128)}, f32[1024,512]{1,0:T(8,128)}) custom-call(f32[2,4,1024,128]{3,2,1,0:T(8,128)S(1)} %get-tuple-element.44.kq_ref, bf16[2,4,1024,256]{3,2,1,0:T(8,128)(2,1)S(1)} %get-tuple-element.45.right_ref, f32[1024,512]{1,0:T(8,128)S(1)} %get-tuple-element.68.old_k, ...), custom_call_target="tpu_custom_call" | custom-call | flops 1000000000 | bytes 8388608 | tf_op jit(solution)/shard_map/back/pallas_call | solution.py:446
  40.3 0.0 collective-permute-done.9
  40.3 0.6 %slice_add_fusion = f32[14,1024]{1,0:T(8,128)} fusion(f32[16,1024]{1,0:T(8,128)S(1)} %collective-permute-done.9, f32[16,1024]{1,0:T(8,128)S(1)} %add.18), kind=kLoop, calls=%fused_computation | loop fusion | flops 14336 | bytes 172032 | tf_op jit(solution)/shard_map/add | solution.py:444
  (4 shorter events, 0.1 us)
Async XLA Ops:
  0.6 11.9 %copy-start = (f32[14,1024]{1,0:T(8,128)S(1)}, f32[14,1024]{1,0:T(8,128)}, u32[]{:S(2)}) copy-start(f32[14,1024]{1,0:T(8,128)} %w_ref.9) | copy-start | bytes 172036
  6.0 5.4 %collective-permute-start.4 = (f32[2,128,128]{2,1,0:T(8,128)S(1)}, f32[2,128,128]{2,1,0:T(8,128)S(1)}, u32[]{:S(2)}, u32[]{:S(2)}) collective-permute-start(f32[2,128,128]{2,1,0:T(8,128)S(1)} %get-tuple-element.78), channel_id=1, source_target_pairs={{0,8},{4,12},{8,0},{12,4},{16,24},{20,28},{24,16},{28,20},{1,9},{5... | collective-permute-start | bytes 393224 | tf_op jit(solution)/shard_map/ppermute | solution.py:21
  8.2 5.7 %collective-permute-start.1 = (f32[2,128,128]{2,1,0:T(8,128)S(1)}, f32[2,128,128]{2,1,0:T(8,128)S(1)}, u32[]{:S(2)}, u32[]{:S(2)}) collective-permute-start(f32[2,128,128]{2,1,0:T(8,128)S(1)} %get-tuple-element.74), channel_id=1, source_target_pairs={{0,4},{4,0},{8,12},{12,8},{16,20},{20,16},{24,28},{28,24},{1,5},{5... | collective-permute-start | bytes 393224 | tf_op jit(solution)/shard_map/ppermute | solution.py:21
  11.4 5.7 %collective-permute-start.5 = (f32[2,128,128]{2,1,0:T(8,128)S(1)}, f32[2,128,128]{2,1,0:T(8,128)S(1)}, u32[]{:S(2)}, u32[]{:S(2)}) collective-permute-start(f32[2,128,128]{2,1,0:T(8,128)S(1)} %add.16), channel_id=1, source_target_pairs={{0,4},{4,0},{8,12},{12,8},{16,20},{20,16},{24,28},{28,24},{1,5},{5... | collective-permute-start | bytes 393224 | tf_op jit(solution)/shard_map/ppermute | solution.py:21
  13.4 13.6 %collective-permute-start = (f32[4,128,128]{2,1,0:T(8,128)S(1)}, f32[4,128,128]{2,1,0:T(8,128)S(1)}, u32[]{:S(2)}, u32[]{:S(2)}) collective-permute-start(f32[4,128,128]{2,1,0:T(8,128)S(1)} %near.1), channel_id=1, source_target_pairs={{0,4},{4,0},{8,12},{12,8},{16,20},{20,16},{24,28},{28,24},{1,5},{5... | collective-permute-start | bytes 786440 | tf_op jit(solution)/shard_map/ppermute | solution.py:21
  13.8 7.5 %collective-permute-start.2 = (f32[2,128,128]{2,1,0:T(8,128)S(1)}, f32[2,128,128]{2,1,0:T(8,128)S(1)}, u32[]{:S(2)}, u32[]{:S(2)}) collective-permute-start(f32[2,128,128]{2,1,0:T(8,128)S(1)} %add.15), channel_id=1, source_target_pairs={{0,8},{4,12},{8,0},{12,4},{16,24},{20,28},{24,16},{28,20},{1,9},{5... | collective-permute-start | bytes 393224 | tf_op jit(solution)/shard_map/ppermute | solution.py:21
  17.1 7.3 %collective-permute-start.6 = (f32[2,128,128]{2,1,0:T(8,128)S(1)}, f32[2,128,128]{2,1,0:T(8,128)S(1)}, u32[]{:S(2)}, u32[]{:S(2)}) collective-permute-start(f32[2,128,128]{2,1,0:T(8,128)S(1)} %add.17), channel_id=1, source_target_pairs={{0,16},{4,20},{8,24},{12,28},{16,0},{20,4},{24,8},{28,12},{1,17},{... | collective-permute-start | bytes 393224 | tf_op jit(solution)/shard_map/ppermute | solution.py:21
  21.3 5.6 %collective-permute-start.3 = (f32[2,128,128]{2,1,0:T(8,128)S(1)}, f32[2,128,128]{2,1,0:T(8,128)S(1)}, u32[]{:S(2)}, u32[]{:S(2)}) collective-permute-start(f32[2,128,128]{2,1,0:T(8,128)S(1)} %collective-permute-done.2.refs_2_), channel_id=1, source_target_pairs={{0,4},{4,0},{8,12},{12,8},{16,20},{20,16},{24,28},{28,24},{1,5},{5... | collective-permute-start | bytes 393224 | tf_op jit(solution)/shard_map/ppermute | solution.py:21
  24.4 5.0 %collective-permute-start.7 = (f32[2,128,128]{2,1,0:T(8,128)S(1)}, f32[2,128,128]{2,1,0:T(8,128)S(1)}, u32[]{:S(2)}, u32[]{:S(2)}) collective-permute-start(f32[2,128,128]{2,1,0:T(8,128)S(1)} %collective-permute-done.6.refs_1_.refs_4_), channel_id=1, source_target_pairs={{0,8},{4,12},{8,0},{12,4},{16,24},{20,28},{24,16},{28,20},{1,9},{5... | collective-permute-start | bytes 393224 | tf_op jit(solution)/shard_map/ppermute | solution.py:21
  30.7 5.1 %collective-permute-start.8 = (f32[16,1024]{1,0:T(8,128)S(1)}, f32[16,1024]{1,0:T(8,128)S(1)}, u32[]{:S(2)}, u32[]{:S(2)}) collective-permute-start(f32[16,1024]{1,0:T(8,128)S(1)} %get-tuple-element.83), channel_id=1, source_target_pairs={{0,1},{1,0},{2,3},{3,2},{4,5},{5,4},{6,7},{7,6},{8,9},{9,8},{10,11... | collective-permute-start | bytes 196616 | tf_op jit(solution)/shard_map/ppermute | solution.py:21
  35.8 4.5 %collective-permute-start.9 = (f32[16,1024]{1,0:T(8,128)S(1)}, f32[16,1024]{1,0:T(8,128)S(1)}, u32[]{:S(2)}, u32[]{:S(2)}) collective-permute-start(f32[16,1024]{1,0:T(8,128)S(1)} %add.18), channel_id=1, source_target_pairs={{0,2},{1,3},{2,0},{3,1},{4,6},{5,7},{6,4},{7,5},{8,10},{9,11},{10,... | collective-permute-start | bytes 196616 | tf_op jit(solution)/shard_map/ppermute | solution.py:21
